TPU v7x, 128 devices: a whole 4x4x4 slice. The times are simulated.
128 devices in a mesh: ent: 32 (over x_hi, z, y), sec: 4 (over x_lo, core).
Axes of the slice: x: 4 (x_hi: 2, x_lo: 2; x = x_hi * 2 + x_lo), y: 4, z: 4, core: 2. Of those that a mesh axis runs over, the one named last changes fastest.
Arguments:
- features: bfloat16 [4096, 256], P('ent'), may hold values from -6 to 6
- theta: bfloat16 [256, 256], replicated, may hold values from -3 to 3
- section_weight: float32 [65536], P(('ent', 'sec')), may hold values from 0.5 to 2
- pair_rows: int32 [128, 32, 512], P(('ent', 'sec')), may hold values from 0 to 511
- pair_cols: int32 [128, 32, 512], P(('ent', 'sec')), may hold values from 0 to 127
- pair_counts: int32 [128, 32], P(('ent', 'sec')), may hold values from 0 to 512, as said below
- cotangent: bfloat16 [4096, 256], P('ent'), may hold values from -24 to 24
Outputs:
- activated: bfloat16 [4096, 256], P('ent')
- grad_features: bfloat16 [4096, 256], P('ent')
- grad_theta: float32 [256, 256], replicated
- grad_weight: float32 [65536], P(('ent', 'sec'))
Inputs may be any that keep to these rules, and one draw needn't show every extreme that they name: Only the first pair_counts[k, j] slots of shard k and block j are used; some shard uses all 512 slots of some block.
All inputs are finite; a program needn't handle non-finite values.
Results may differ from a plain program's by a relative error of at most 0.0059.
Values may be sent and summed in bfloat16 or wider, within the bound.
A program may use at most 64 MiB of HBM per device.

v0:
```python
import jax
import jax.numpy as jnp
from jax import lax
from jax.sharding import PartitionSpec as P


def hot_table(indices, live_slots, offset, table_width):
    hits = (indices - offset)[:, None] == jnp.arange(table_width, dtype=jnp.int32)[None, :]
    return (hits & live_slots[:, None]).astype(jnp.bfloat16)


def body(features, theta, section_weight, pair_rows, pair_cols, pair_counts, cotangent):
    ent_dev = features.shape[0]
    feature_width = features.shape[1]
    sec_dev = section_weight.shape[0]
    blocks_count = pair_rows.shape[1]
    slot_count = pair_rows.shape[2]
    own_block = lax.axis_index("ent")
    row_lists = pair_rows[0]
    col_lists = pair_cols[0]
    usable = jnp.arange(slot_count, dtype=jnp.int32)[None, :] < pair_counts[0][:, None]
    usable_float = usable.astype(jnp.float32)
    entity_index = jnp.arange(blocks_count, dtype=jnp.int32)[:, None] * ent_dev + col_lists
    local_degree = jax.ops.segment_sum(
        usable_float.reshape(-1), entity_index.reshape(-1), num_segments=blocks_count * ent_dev
    )
    entity_degree = lax.psum(local_degree, ("ent", "sec"))
    own_degree = lax.dynamic_slice_in_dim(entity_degree, own_block * ent_dev, ent_dev)
    entity_scale = lax.rsqrt(1.0 + own_degree)[:, None]
    sec_count = jax.ops.segment_sum(
        usable_float.reshape(-1), row_lists.reshape(-1), num_segments=sec_dev
    )
    section_scale = (section_weight / (1.0 + sec_count))[:, None]

    def entity_fold(running, incoming, start_row):
        row_count = incoming.shape[0]
        span_width = min(row_count, ent_dev)
        block_span = max(row_count // ent_dev, 1)
        offset = start_row

        def add_block(turn_index, accum):
            row_slots = lax.dynamic_index_in_dim(row_lists, turn_index, 0, keepdims=False)
            col_slots = lax.dynamic_index_in_dim(col_lists, turn_index, 0, keepdims=False)
            live_slots = lax.dynamic_index_in_dim(usable, turn_index, 0, keepdims=False)
            values = lax.dynamic_slice_in_dim(incoming, turn_index * span_width, span_width, 0)
            col_hot = hot_table(col_slots, live_slots, offset, span_width)
            row_hot = hot_table(row_slots, live_slots, 0, sec_dev)
            picked = jnp.dot(col_hot, values, preferred_element_type=jnp.float32).astype(
                jnp.bfloat16
            )
            return accum + jnp.einsum(
                "ps,pf->sf", row_hot, picked, preferred_element_type=jnp.float32
            )

        return lax.fori_loop(0, block_span, add_block, running)

    def entity_terms(messages, start_row):
        span_width = min(lax.axis_size("ent") * ent_dev, ent_dev)
        block_span = max(lax.axis_size("ent") * ent_dev // ent_dev, 1)
        offset = start_row

        def block_term(turn_index):
            row_slots = lax.dynamic_index_in_dim(row_lists, turn_index, 0, keepdims=False)
            col_slots = lax.dynamic_index_in_dim(col_lists, turn_index, 0, keepdims=False)
            live_slots = lax.dynamic_index_in_dim(usable, turn_index, 0, keepdims=False)
            row_hot = hot_table(row_slots, live_slots, 0, sec_dev)
            col_hot = hot_table(col_slots, live_slots, offset, span_width)
            picked = jnp.dot(row_hot, messages, preferred_element_type=jnp.float32).astype(
                jnp.bfloat16
            )
            return jnp.einsum("pw,pf->wf", col_hot, picked, preferred_element_type=jnp.float32)

        pieces = lax.map(block_term, jnp.arange(block_span, dtype=jnp.int32))
        return pieces.reshape(block_span * span_width, feature_width)

    def collect(messages):
        partial_sum = lax.psum_scatter(
            entity_terms(messages, jnp.int32(0)), "ent", scatter_dimension=0, tiled=True
        )
        return lax.psum(partial_sum, "sec")

    zero_sections = jnp.zeros((sec_dev, feature_width), jnp.float32)
    projected = jnp.dot(features, theta, preferred_element_type=jnp.float32)
    scaled = (entity_scale * projected).astype(jnp.bfloat16)
    gathered = entity_fold(
        zero_sections, lax.all_gather(scaled, "ent", axis=0, tiled=True), jnp.int32(0)
    )
    messages = (section_scale * gathered).astype(jnp.bfloat16)
    collected = collect(messages)
    preact = entity_scale * collected
    activated = jax.nn.silu(preact).astype(jnp.bfloat16)
    sigmoid_pre = jax.nn.sigmoid(preact)
    grad_pre = cotangent.astype(jnp.float32) * sigmoid_pre * (1.0 + preact * (1.0 - sigmoid_pre))
    back_scaled = (entity_scale * grad_pre).astype(jnp.bfloat16)
    back_gathered = entity_fold(
        zero_sections, lax.all_gather(back_scaled, "ent", axis=0, tiled=True), jnp.int32(0)
    )
    grad_weight = jnp.sum(gathered * back_gathered, axis=1) / (1.0 + sec_count)
    back_messages = (section_scale * back_gathered).astype(jnp.bfloat16)
    back_collected = collect(back_messages)
    grad_proj = (entity_scale * back_collected).astype(jnp.bfloat16)
    grad_features = lax.dot_general(
        grad_proj, theta, (((1,), (1,)), ((), ())), preferred_element_type=jnp.float32
    ).astype(jnp.bfloat16)
    local_theta = lax.dot_general(
        features, grad_proj, (((0,), (0,)), ((), ())), preferred_element_type=jnp.float32
    )
    grad_theta = lax.psum(local_theta, "ent")
    return (activated, grad_features, grad_theta, grad_weight)


def solution(mesh):
    placed = (
        P("ent", None),
        P(),
        P(("ent", "sec")),
        P(("ent", "sec"), None, None),
        P(("ent", "sec"), None, None),
        P(("ent", "sec"), None),
        P("ent", None),
    )
    return jax.shard_map(
        body,
        mesh=mesh,
        in_specs=placed,
        out_specs=(P("ent", None), P("ent", None), P(), P(("ent", "sec"))),
        check_vma=False,
    )
```

profile of v0, /device:TPU:0, one launch (start us, length us, event | category | flops | bytes accessed | tf_op | source)
XLA Modules:
  0.0 1644.0 jit_solution(5554662827985014451)
XLA Ops:
  9.2 113.5 %scatter_custom_fusion = f32[4096]{0:T(1024)S(1)} fusion(s32[16384]{0:T(1024)S(1)} %bitcast.81, f32[16384]{0:T(1024)S(1)} %bitcast.82, f32[]{:T(128)} %constant.131.clone.1), kind=kCustom, calls=%fused_computation.76 | custom fusion | flops 16384 | bytes 16388 | tf_op jit(solution)/shard_map/scatter-add | solution.py:24
  122.6 68.3 %psum.28 = f32[4096]{0:T(1024)S(1)} all-reduce(f32[4096]{0:T(1024)S(1)} %scatter_custom_fusion), channel_id=1, replica_groups=mesh['ent'=32,'sec'=4] {'ent','sec'}, use_global_device_ids=true, to_apply=%region_1.0 | all-reduce | flops 4096 | bytes 32768 | tf_op jit(solution)/shard_map/psum | solution.py:27
  193.5 113.4 %scatter_custom_fusion.1 = f32[512]{0:T(512)S(1)} fusion(s32[16384]{0:T(1024)S(1)} %bitcast.84, f32[16384]{0:T(1024)S(1)} %bitcast.83, f32[]{:T(128)} %constant.137.clone.1), kind=kCustom, calls=%fused_computation.78 | custom fusion | flops 16384 | bytes 2052 | tf_op jit(solution)/shard_map/scatter-add | solution.py:30
  307.7 79.9 %while.50 = (s32[]{:T(128)}, f32[512,256]{1,0:T(8,128)S(1)}, s32[32,512]{1,0:T(8,128)}, pred[32,512]{1,0:T(8,128)(4,1)S(1)}, s32[32,512]{1,0:T(8,128)}, /*index=...) while((s32[]{:T(128)}, f32[512,256]{1,0:T(8,128)S(1)}, ...), condition=%wide.region_4.5_spmd.clone, body=%wide.region_3.4_spmd.clone.sunk | while | flops 168820736 | bytes 1128617 | solution.py:55
  313.4 1.7 convolution_add_fusion.4
  315.9 1.7 convolution_add_fusion.4
  320.9 1.7 convolution_add_fusion.4
  323.4 1.7 convolution_add_fusion.4
  325.9 1.7 convolution_add_fusion.4
  330.9 1.7 convolution_add_fusion.4
  333.4 1.7 convolution_add_fusion.4
  335.9 1.7 convolution_add_fusion.4
  338.4 1.7 convolution_add_fusion.4
  340.9 1.7 convolution_add_fusion.4
  343.4 1.7 convolution_add_fusion.4
  348.4 1.7 convolution_add_fusion.4
  350.9 1.7 convolution_add_fusion.4
  353.4 1.7 convolution_add_fusion.4
  358.4 1.7 convolution_add_fusion.4
  360.9 1.7 convolution_add_fusion.4
  365.9 1.7 convolution_add_fusion.4
  368.4 1.7 convolution_add_fusion.4
  383.4 1.7 convolution_add_fusion.4
  385.9 1.7 convolution_add_fusion.4
  387.7 2.4 broadcast.21.clone
  390.2 144.5 %while.48 = (s32[]{:T(128)}, f32[32,128,256]{2,1,0:T(8,128)}, s32[32]{0:T(128)S(1)}, s32[32,512]{1,0:T(8,128)}, pred[32,512]{1,0:T(8,128)(4,1)S(1)}, /*index=5*/...) while((s32[]{:T(128)}, f32[32,128,256]{2,1,0:T(8,128)}, ...), condition=%wide.region_6.7_spmd, body=%wide.region_5.6_spmd.sunk | while | flops 168558592 | bytes 408219 | solution.py:73
  534.8 188.6 %reduce-scatter.3.cloned.1.call-done = f32[128,256]{1,0:T(8,128)} async-done(((f32[4096,256]{1,0:T(8,128)}), f32[128,256]{1,0:T(8,128)}) %reduce-scatter.3.cloned.1.call-update) | async-done | bytes 131088 | tf_op jit(solution)/shard_map/reduce_scatter | solution.py:77
  723.4 32.8 %all-reduce.4.cloned.1.call-done = f32[128,256]{1,0:T(8,128)} async-done(((f32[128,256]{1,0:T(8,128)}), f32[128,256]{1,0:T(8,128)}) %all-reduce.4.cloned.1.call-update) | async-done | bytes 131088 | tf_op jit(solution)/shard_map/psum | solution.py:80
  756.2 1.7 multiply_convert_fusion.3
  758.0 73.9 %all-gather.5.cloned.1.call-done = bf16[4096,256]{1,0:T(8,128)(2,1)} async-done(((bf16[128,256]{1,0:T(8,128)(2,1)}), bf16[4096,256]{1,0:T(8,128)(2,1)}) %all-gather.5.cloned.1.call-update) | async-done | bytes 2097168 | tf_op jit(solution)/shard_map/all_gather | solution.py:96
  831.9 79.9 %while.51 = (s32[]{:T(128)}, f32[512,256]{1,0:T(8,128)S(1)}, s32[32,512]{1,0:T(8,128)}, pred[32,512]{1,0:T(8,128)(4,1)S(1)}, s32[32,512]{1,0:T(8,128)}, /*index=...) while((s32[]{:T(128)}, f32[512,256]{1,0:T(8,128)S(1)}, ...), condition=%wide.region_10.11_spmd.clone, body=%wide.region_9.10_spmd.clone.sunk | while | flops 168820736 | bytes 1128617 | solution.py:55
  832.6 1.7 convolution_add_fusion.5
  842.6 1.7 convolution_add_fusion.5
  845.1 1.7 convolution_add_fusion.5
  860.1 1.7 convolution_add_fusion.5
  862.6 1.7 convolution_add_fusion.5
  877.6 1.7 convolution_add_fusion.5
  880.1 1.7 convolution_add_fusion.5
  895.1 1.7 convolution_add_fusion.5
  897.6 1.7 convolution_add_fusion.5
  912.0 2.4 broadcast.21
  914.4 144.5 %while.49 = (s32[]{:T(128)}, f32[32,128,256]{2,1,0:T(8,128)}, s32[32]{0:T(128)S(1)}, s32[32,512]{1,0:T(8,128)}, pred[32,512]{1,0:T(8,128)(4,1)S(1)}, /*index=5*/...) while((s32[]{:T(128)}, f32[32,128,256]{2,1,0:T(8,128)}, ...), condition=%wide.region_12.13_spmd, body=%wide.region_11.12_spmd.sunk | while | flops 168558592 | bytes 408219 | solution.py:73
  1059.0 190.6 %reduce-scatter.5.cloned.1.call-done = f32[128,256]{1,0:T(8,128)} async-done(((f32[4096,256]{1,0:T(8,128)}), f32[128,256]{1,0:T(8,128)}) %reduce-scatter.5.cloned.1.call-update) | async-done | bytes 131088 | tf_op jit(solution)/shard_map/reduce_scatter | solution.py:77
  1249.7 32.8 %all-reduce.6.cloned.1.call-done = f32[128,256]{1,0:T(8,128)} async-done(((f32[128,256]{1,0:T(8,128)}), f32[128,256]{1,0:T(8,128)}) %all-reduce.6.cloned.1.call-update) | async-done | bytes 131088 | tf_op jit(solution)/shard_map/psum | solution.py:80
  1282.5 1.9 convolution_bitcast_fusion
  1285.0 1.7 convolution_convert_fusion.4
  1286.8 348.6 %all-reduce.8.cloned.1.call-done = f32[256,256]{0,1:T(8,128)} async-done(((f32[256,256]{0,1:T(8,128)}), f32[256,256]{0,1:T(8,128)}) %all-reduce.8.cloned.1.call-update) | async-done | bytes 262160 | tf_op jit(solution)/shard_map/psum | solution.py:108
  1635.4 1.8 copy.11
  (458 shorter events, 279.9 us)
Async XLA Ops:
  7.2 183.8 %copy-start = (bf16[256,256]{1,0:T(8,128)(2,1)S(1)}, bf16[256,256]{1,0:T(8,128)(2,1)}, u32[]{:S(2)}) copy-start(bf16[256,256]{1,0:T(8,128)(2,1)} %param.16) | copy-start | bytes 393220
  7.2 300.5 %all-gather.3.cloned.1.call-start = ((), (), s32[]{:S(2)}) async-start(), calls=%async_computation.2 | async-start | bytes 2162688 | tf_op jit(solution)/shard_map/all_gather | solution.py:86
  192.6 530.7 %reduce-scatter.3.cloned.1.call-start = ((), (), s32[]{:S(2)}) async-start(), calls=%async_computation.3 | async-start | bytes 4325376 | tf_op jit(solution)/shard_map/reduce_scatter | solution.py:77
  390.1 366.0 %copy-start.2 = (bf16[128,256]{1,0:T(8,128)(2,1)S(1)}, bf16[128,256]{1,0:T(8,128)(2,1)}, u32[]{:S(2)}) copy-start(bf16[128,256]{1,0:T(8,128)(2,1)} %param.21) | copy-start | bytes 196612
  534.7 221.5 %all-reduce.4.cloned.1.call-start = ((), (), s32[]{:S(2)}) async-start(), calls=%async_computation.4 | async-start | bytes 262144 | tf_op jit(solution)/shard_map/psum | solution.py:80
  723.4 108.5 %all-gather.5.cloned.1.call-start = ((), (), s32[]{:S(2)}) async-start(), calls=%async_computation.5 | async-start | bytes 2162688 | tf_op jit(solution)/shard_map/all_gather | solution.py:96
  757.9 491.7 %reduce-scatter.5.cloned.1.call-start = ((), (), s32[]{:S(2)}) async-start(), calls=%async_computation.6 | async-start | bytes 4325376 | tf_op jit(solution)/shard_map/reduce_scatter | solution.py:77
  914.4 368.1 %copy-start.1 = (bf16[128,256]{1,0:T(8,128)(2,1)S(1)}, bf16[128,256]{1,0:T(8,128)(2,1)}, u32[]{:S(2)}) copy-start(bf16[128,256]{1,0:T(8,128)(2,1)} %param.15) | copy-start | bytes 196612
  1059.0 223.6 %all-reduce.6.cloned.1.call-start = ((), (), s32[]{:S(2)}) async-start(), calls=%async_computation.7 | async-start | bytes 262144 | tf_op jit(solution)/shard_map/psum | solution.py:80
  1249.7 385.8 %all-reduce.8.cloned.1.call-start = ((), (), s32[]{:S(2)}) async-start(), calls=%async_computation.8 | async-start | bytes 524288 | tf_op jit(solution)/shard_map/psum | solution.py:108
Sparse Core Ops, SparseCore 0:
  192.7 66.8 all-gather.2
  534.8 188.4 reduce-scatter.2
  725.8 30.3 all-reduce.3
  760.1 71.6 all-gather.4
  1059.1 190.4 reduce-scatter.4
  1252.1 30.3 all-reduce.5
  1285.6 349.7 all-reduce.7
where the time goes:
time: 1670 us; the launch traced here: 1640 us
  waiting for transfers between devices  867 us (52%)
  other arithmetic  231 us (14%)
  matrix products  191 us (11%)
  local copies, waits for them, and re-layouts  145 us (9%)
  loops' own time  126 us (8%)
  blocking collectives  68.3 us (4%)
    reduce_scatter x2, waiting for transfers between devices, collect(): lax.psum_scatter(entity_terms(messages, jnp.int32(0)), 'ent', scatter_dim...  379 us
    psum x1, waiting for transfers between devices, body(): grad_theta = lax.psum(local_theta, 'ent')  349 us
    another operation x2, loops' own time, entity_terms(): pieces = lax.map(block_term, jnp.arange(block_span, dtype=jnp.int32))  125 us
    scatter-add x1, other arithmetic, body(): jax.ops.segment_sum(usable_float.reshape(-1), entity_index.reshape(-1), n...  113 us
    scatter-add x1, other arithmetic, body(): jax.ops.segment_sum(usable_float.reshape(-1), row_lists.reshape(-1), num_...  113 us
    dot_general x64, matrix products, add_block(): jnp.einsum('ps,pf->sf', row_hot, picked, preferred_element_type=jnp.float32)  108 us
    dot_general x64, matrix products, block_term(): jnp.einsum('pw,pf->wf', col_hot, picked, preferred_element_type=jnp.float32)  77.7 us
    all_gather x1, waiting for transfers between devices, body(): lax.all_gather(back_scaled, 'ent', axis=0, tiled=True)  73.9 us
  transfers between devices with their start and end apart: 7, of which 6 were waited for; matrix products, arithmetic and copies ran while one was open for 7% of the time, Pallas kernels for 0%

commit v1 on v0

v1 whole, which is shorter than its diff:
```python
import jax
import jax.numpy as jnp
from jax import lax
from jax.experimental import pallas as pl
from jax.experimental.pallas import tpu as pltpu
from jax.sharding import PartitionSpec as P

F32 = jnp.float32
BF16 = jnp.bfloat16
MESH = pl.DeviceIdType.MESH
NT = (((1,), (1,)), ((), ()))
NN = (((1,), (0,)), ((), ()))
N_SEM = 160


def dot(a, b, dims):
    return lax.dot_general(a, b, dims, preferred_element_type=F32)


def split(v):
    hi = v.astype(BF16)
    return hi, (v - hi.astype(F32)).astype(BF16)


def layer(
    feat, theta, sw, rows, cols, counts, cot,
    act_o, gf_o, gt_o, gw_o,
    HT, HS, degs, degr, degc, degt, SW, INV, XF, XS, G, GR, GH, GL, GATH, MT, PF, PB,
    RB, CB, ACC, YS, YR, A2, XR, AS, AR, FS, FR, TH,
    T0, TZ, T1, TY, TX, T3, TS, ssem, rsem,
):
    e = lax.axis_index("ent")
    s = lax.axis_index("sec")
    core = lax.rem(s, 2)
    xl = lax.div(s, 2)
    xh = lax.div(e, 16)
    z = lax.rem(lax.div(e, 4), 4)
    y = lax.rem(e, 4)
    myx = xh * 2 + xl
    half = pl.multiple_of(core * 64, 64)
    other_half = pl.multiple_of((1 - core) * 64, 64)

    def dev(xh_, xl_, z_, y_):
        return (xh_ * 16 + z_ * 4 + y_, xl_ * 2 + core)

    sib = (e, xl * 2 + 1 - core)
    x_pair = dev(1 - xh, 1 - xl, z, y)
    x_far = dev(1 - xh, xl, z, y)
    x_same = dev(xh, 1 - xl, z, y)

    def mod4(v):
        return lax.rem(v + 4, 4)

    def z_dev(d):
        return dev(xh, xl, mod4(z + d), y)

    def y_dev(d):
        return dev(xh, xl, z, mod4(y + d))

    peers = [sib, x_pair, x_far, x_same] + [z_dev(d) for d in (1, 2, 3)] + [y_dev(d) for d in (1, 2, 3)]
    sent = []

    def send(src, dst, device):
        i = len(sent)
        copy = pltpu.make_async_remote_copy(
            src_ref=src, dst_ref=dst, send_sem=ssem.at[i], recv_sem=rsem.at[i],
            device_id=device, device_id_type=MESH,
        )
        copy.start()
        sent.append(copy)
        return copy

    def arrived(copies):
        for copy in copies:
            copy.wait_recv()

    barrier = pltpu.get_barrier_semaphore()
    for peer in peers:
        pl.semaphore_signal(barrier, inc=1, device_id=peer, device_id_type=MESH)

    slot_row = lax.broadcasted_iota(jnp.int32, (1, 512), 1)
    ent_iota = lax.broadcasted_iota(jnp.int32, (128, 512), 0)

    def col_table(j):
        live = slot_row < counts[0, j]
        col = jnp.where(live, cols[0, pl.ds(j, 1), :], -1)
        return jnp.where(ent_iota == col, 1.0, 0.0).astype(BF16)

    for p in range(2):
        XF[0, p, xh, z, y] = feat[pl.ds(half, 64), p * 128:(p + 1) * 128]
    TH[...] = theta[...].T

    pl.semaphore_wait(barrier, len(peers))

    def all_gather(ph, p):
        buf = XF.at[ph, p]
        axis_dev, ring_dev, ring = (y_dev, z_dev, z) if p == 0 else (z_dev, y_dev, y)

        def line(i):
            return buf.at[:, i] if p == 0 else buf.at[:, :, i]

        def part_line(i, lo):
            return buf.at[:, i, lo:lo + 2] if p == 0 else buf.at[:, lo:lo + 2, i]

        own = buf.at[xh, z, y]
        m = [send(own, own, x_pair)]
        yield
        arrived(m)
        own = buf.at[:, z, y]
        m = [send(own, own, axis_dev(d)) for d in (1, 3, 2)]
        yield
        arrived(m)
        m = [send(line(ring), line(ring), ring_dev(d)) for d in (1, 3)]
        yield
        arrived(m)
        below, above = mod4(ring - 1), mod4(ring + 1)
        m = [
            send(part_line(below, 0), part_line(below, 0), ring_dev(1)),
            send(part_line(above, 2), part_line(above, 2), ring_dev(3)),
        ]
        yield
        arrived(m)
        yield

    def degree_sum():
        m = [send(degs.at[0], degr.at[0], sib)]
        yield
        arrived(m)
        degs[1] = degs[0] + degr[0]
        m = [send(degs.at[1], degr.at[1 + i], d) for i, d in enumerate((x_pair, x_same, x_far))]
        yield
        arrived(m)
        degs[2] = degs[1] + degr[1] + degr[2] + degr[3]
        m = [send(degs.at[2], degr.at[3 + d], y_dev(d)) for d in (1, 3, 2)]
        yield
        arrived(m)
        degs[3] = degs[2] + degr[4] + degr[5] + degr[6]
        m = [send(degs.at[3], degr.at[6 + d], z_dev(d)) for d in (1, 3, 2)]
        yield
        arrived(m)
        degs[4] = degs[3] + degr[7] + degr[8] + degr[9]
        yield

    def step(gens):
        for g in gens:
            next(g, None)

    gathers = [all_gather(0, 0), all_gather(0, 1)]
    step(gathers)
    SW[0] = sw[...]
    sw_copy = send(SW.at[0], SW.at[1], sib)

    ones = jnp.ones((8, 512), BF16)

    def degree_block(j, carry):
        degs[0, pl.ds(j, 1), :] = dot(ones, col_table(j), NT)[0:1]
        return carry

    lax.fori_loop(0, 32, degree_block, 0)
    degrees = degree_sum()
    step([degrees] + gathers)

    sec_iota = lax.broadcasted_iota(jnp.int32, (512, 512), 0)

    def table_block(j, carry):
        row_hot = jnp.where(sec_iota == rows[0, pl.ds(j, 1), :], 1.0, 0.0).astype(BF16)
        block = dot(col_table(j), row_hot, NT).astype(BF16)
        HT[0, j] = block[0:64]
        HT[1, j] = block[64:128]
        return carry

    table_copies = []
    for k in range(8):
        lax.fori_loop(4 * k, 4 * k + 4, table_block, 0)
        table_copies.append(send(HT.at[1 - core, 4 * k:4 * k + 4], HS.at[4 * k:4 * k + 4], sib))
        step([degrees] + gathers)

    arrived(table_copies)
    arrived([sw_copy])

    degc[...] = jnp.zeros((128, 128), F32)
    degc[0:32, :] = lax.rsqrt(1.0 + degs[4])
    degt[...] = degc[...].T
    scales = degt[pl.ds(half, 64), :]
    own_lane = lax.broadcasted_iota(jnp.int32, (64, 128), 1) == e
    own_scale = jnp.sum(jnp.where(own_lane, scales, 0.0), axis=1, keepdims=True)

    for j in range(32):
        for p in range(2):
            v = XF[0, p, j // 16, (j // 4) % 4, j % 4].astype(F32)
            XS[p, j // 4, j % 4] = (v * scales[:, j:j + 1]).astype(BF16)

    def gather_sections(ph):
        width = 272 if ph == 0 else 256
        for k in range(2):
            G[ph, k, 0:width] = jnp.zeros((width, 512), F32)

        def chunk(kk, carry):
            if ph == 0:
                pieces = [XS[p, kk].reshape(256, 128) for p in range(2)]
            else:
                pieces = [XF[1, p, lax.div(kk, 4), lax.rem(kk, 4)].reshape(256, 128) for p in range(2)]
            xt = jnp.concatenate(pieces, axis=1).T
            if ph == 0:
                xt = jnp.concatenate([xt, jnp.ones((16, 256), BF16)], axis=0)
            own = HT[core, pl.ds(4 * kk, 4)].reshape(256, 512)
            sibs = HS[pl.ds(4 * kk, 4)].reshape(256, 512)
            G[ph, 0, 0:width] += dot(xt, own, NN)
            G[ph, 1, 0:width] += dot(xt, sibs, NN)
            return carry

        lax.fori_loop(0, 8, chunk, 0)
        m = [send(G.at[ph, k, 0:width], GR.at[ph, k, 0:width], sib) for k in (1, 0)]
        arrived(m)
        return [G[ph, k, 0:width] + GR[ph, 1 - k, 0:width] for k in range(2)]

    def scatter_entities(ph):
        def chunk(kk, carry):
            own = HT[core, pl.ds(4 * kk, 4)].reshape(256, 512)
            sibs = HS[pl.ds(4 * kk, 4)].reshape(256, 512)
            v = dot(own, MT[ph, 0], NT) + dot(sibs, MT[ph, 1], NT)
            a, b = lax.div(kk, 4), lax.rem(kk, 4)
            for p in range(2):
                piece = v[:, p * 128:(p + 1) * 128].reshape(4, 64, 128)
                PF[p, a, b] = piece
                PB[ph, p, a, b] = piece.astype(BF16)
            return carry

        lax.fori_loop(0, 8, chunk, 0)

    def reduce_scatter(ph, p, out):
        full, low = PF.at[p], PB.at[ph, p]
        ring_dev, axis_dev, ring, axis = (z_dev, y_dev, z, y) if p == 0 else (y_dev, z_dev, y, z)

        def lines(ref, i, lo):
            return ref.at[:, i, lo:lo + 2] if p == 0 else ref.at[:, lo:lo + 2, i]

        def tile(a, i, o):
            return full[a, i, o] if p == 0 else full[a, o, i]

        far, above, below = mod4(ring + 2), mod4(ring + 1), mod4(ring - 1)
        rb, cb = RB.at[ph, p], CB.at[ph, p]
        far_up = send(lines(low, far, 0), rb.at[0], ring_dev(1))
        far_down = send(lines(low, far, 2), rb.at[1], ring_dev(3))
        near_up = send(lines(low, above, 2), rb.at[2], ring_dev(1))
        near_down = send(lines(low, below, 0), rb.at[3], ring_dev(3))
        yield
        arrived([far_up])
        for a in range(2):
            for o in range(2):
                cb[0, a, o] = (tile(a, above, o) + rb[0, a, o].astype(F32)).astype(BF16)
        up = send(cb.at[0], rb.at[4], ring_dev(1))
        arrived([far_down])
        for a in range(2):
            for o in range(2):
                cb[1, a, o] = (tile(a, below, 2 + o) + rb[1, a, o].astype(F32)).astype(BF16)
        down = send(cb.at[1], rb.at[5], ring_dev(3))
        yield
        arrived([near_up, near_down, up, down])
        for a in range(2):
            for o in range(2):
                low_sum = tile(a, ring, o) + rb[3, a, o].astype(F32) + rb[4, a, o].astype(F32)
                high_sum = tile(a, ring, 2 + o) + rb[2, a, o].astype(F32) + rb[5, a, o].astype(F32)
                ACC[p, o, a] = low_sum
                ACC[p, 2 + o, a] = high_sum
                YS[ph, p, o, a] = low_sum.astype(BF16)
                YS[ph, p, 2 + o, a] = high_sum.astype(BF16)
        m = [send(YS.at[ph, p, mod4(axis + d)], YR.at[ph, p, d - 1], axis_dev(d)) for d in (2, 1, 3)]
        yield
        arrived(m)
        for a in range(2):
            v = ACC[p, axis, a]
            for i in range(3):
                v = v + YR[ph, p, i, a].astype(F32)
            A2[ph, p, a] = v
        m = [
            send(A2.at[ph, p, 1 - xh], XR.at[ph, p, myx], x_far),
            send(A2.at[ph, p, 1 - xh], XR.at[ph, p, myx], x_pair),
            send(A2.at[ph, p, xh], XR.at[ph, p, myx], x_same),
        ]
        XR[ph, p, myx] = A2[ph, p, xh]
        yield
        arrived(m)
        out[p] = (XR[ph, p, 0] + XR[ph, p, 1]) + (XR[ph, p, 2] + XR[ph, p, 3])
        yield

    totals = gather_sections(0)
    for k in range(2):
        g = totals[k]
        inverse = 1.0 / (1.0 + g[256:257])
        hi, lo = split(g[0:256])
        GH[k] = hi
        GL[k] = lo
        gathered = dot(TH[...], hi, NN) + dot(TH[...], lo, NN)
        if k == 0:
            GATH[...] = gathered
        INV[k] = inverse
        MT[0, k] = ((SW[k] * inverse) * gathered).astype(BF16)
    scatter_entities(0)

    collected = {}
    flows = [reduce_scatter(0, p, collected) for p in range(2)]
    for _ in range(5):
        step(flows)

    back = []
    for p in range(2):
        lanes = slice(p * 128, (p + 1) * 128)
        preact = own_scale * collected[p]
        sig = 1.0 / (1.0 + jnp.exp(-preact))
        AS[:, lanes] = (preact * sig).astype(BF16)
        grad = cot[pl.ds(half, 64), lanes].astype(F32) * sig * (1.0 + preact * (1.0 - sig))
        XF[1, p, xh, z, y] = (own_scale * grad).astype(BF16)
        back.append(all_gather(1, p))
        step([back[p]])
    act_copy = send(AS, AR, sib)
    for _ in range(4):
        step(back)
    act_o[pl.ds(half, 64), :] = AS[...]
    arrived([act_copy])
    act_o[pl.ds(other_half, 64), :] = AR[...]

    totals = gather_sections(1)
    for k in range(2):
        g = totals[k]
        if k == 0:
            gw_o[...] = jnp.sum(GATH[...] * g, axis=0, keepdims=True) * INV[0]
        MT[1, k] = ((SW[k] * INV[k]) * g).astype(BF16)
    scatter_entities(1)

    def theta_sum():
        rows_here = pl.ds(pl.multiple_of(core * 128, 128), 128)
        v = jnp.zeros((128, 256), F32)
        for k in range(2):
            v = v + dot(GH[k, rows_here, :], MT[1, k], NT) + dot(GL[k, rows_here, :], MT[1, k], NT)
        T0[...] = v.reshape(4, 4, 8, 256)
        m = [send(T0.at[mod4(z + d)], TZ.at[d - 1], z_dev(d)) for d in (2, 1, 3)]
        yield
        arrived(m)
        T1[...] = T0[z] + TZ[0] + TZ[1] + TZ[2]
        m = [send(T1.at[mod4(y + d)], TY.at[d - 1], y_dev(d)) for d in (2, 1, 3)]
        yield
        arrived(m)
        TX[myx] = T1[y] + TY[0] + TY[1] + TY[2]
        m = [send(TX.at[myx], TX.at[myx], d) for d in (x_far, x_pair, x_same)]
        yield
        arrived(m)
        T3[z, y] = (TX[0] + TX[1]) + (TX[2] + TX[3])
        m = [send(T3.at[z, y], T3.at[z, y], y_dev(d)) for d in (2, 1, 3)]
        yield
        arrived(m)
        m = [send(T3.at[z], T3.at[z], z_dev(d)) for d in (2, 1, 3)]
        yield
        arrived(m)
        m = [send(T3, TS, sib)]
        yield
        arrived(m)
        mine = pl.ds(pl.multiple_of(core * 128, 128), 128)
        theirs = pl.ds(pl.multiple_of((1 - core) * 128, 128), 128)
        gt_o[mine, :] = T3[...].reshape(128, 256)
        gt_o[theirs, :] = TS[...].reshape(128, 256)
        yield

    collected = {}
    flows = [reduce_scatter(1, p, collected) for p in range(2)]
    step(flows)
    flows.append(theta_sum())
    step(flows[2:])
    for _ in range(4):
        step(flows)

    proj = jnp.concatenate([own_scale * collected[p] for p in range(2)], axis=1)
    hi, lo = split(proj)
    FS[...] = (dot(hi, theta[...], NT) + dot(lo, theta[...], NT)).astype(BF16)
    grad_copy = send(FS, FR, sib)
    step(flows)
    gf_o[pl.ds(half, 64), :] = FS[...]
    arrived([grad_copy])
    gf_o[pl.ds(other_half, 64), :] = FR[...]
    step(flows)
    step(flows)
    assert len(sent) <= N_SEM
    for copy in sent:
        copy.wait_send()


def body(features, theta, section_weight, pair_rows, pair_cols, pair_counts, cotangent):
    vmem = pl.BlockSpec(memory_space=pltpu.VMEM)
    smem = pl.BlockSpec(memory_space=pltpu.SMEM)

    def buf(shape, dtype):
        return pltpu.VMEM(shape, dtype)

    outs = pl.pallas_call(
        layer,
        out_shape=(
            jax.ShapeDtypeStruct((128, 256), BF16),
            jax.ShapeDtypeStruct((128, 256), BF16),
            jax.ShapeDtypeStruct((256, 256), F32),
            jax.ShapeDtypeStruct((1, 512), F32),
        ),
        in_specs=[vmem, vmem, vmem, vmem, vmem, smem, vmem],
        out_specs=(vmem, vmem, vmem, vmem),
        scratch_shapes=[
            buf((2, 32, 64, 512), BF16),
            buf((32, 64, 512), BF16),
            buf((5, 32, 128), F32),
            buf((10, 32, 128), F32),
            buf((128, 128), F32),
            buf((128, 128), F32),
            buf((2, 1, 512), F32),
            buf((2, 1, 512), F32),
            buf((2, 2, 2, 4, 4, 64, 128), BF16),
            buf((2, 8, 4, 64, 128), BF16),
            buf((2, 2, 272, 512), F32),
            buf((2, 2, 272, 512), F32),
            buf((2, 256, 512), BF16),
            buf((2, 256, 512), BF16),
            buf((256, 512), F32),
            buf((2, 2, 256, 512), BF16),
            buf((2, 2, 4, 4, 64, 128), F32),
            buf((2, 2, 2, 4, 4, 64, 128), BF16),
            buf((2, 2, 6, 2, 2, 64, 128), BF16),
            buf((2, 2, 2, 2, 2, 64, 128), BF16),
            buf((2, 4, 2, 64, 128), F32),
            buf((2, 2, 4, 2, 64, 128), BF16),
            buf((2, 2, 3, 2, 64, 128), BF16),
            buf((2, 2, 2, 64, 128), F32),
            buf((2, 2, 4, 64, 128), F32),
            buf((64, 256), BF16),
            buf((64, 256), BF16),
            buf((64, 256), BF16),
            buf((64, 256), BF16),
            buf((256, 256), BF16),
            buf((4, 4, 8, 256), F32),
            buf((3, 4, 8, 256), F32),
            buf((4, 8, 256), F32),
            buf((3, 8, 256), F32),
            buf((4, 8, 256), F32),
            buf((4, 4, 8, 256), F32),
            buf((4, 4, 8, 256), F32),
            pltpu.SemaphoreType.DMA((N_SEM,)),
            pltpu.SemaphoreType.DMA((N_SEM,)),
        ],
        compiler_params=pltpu.CompilerParams(
            collective_id=0, has_side_effects=True, vmem_limit_bytes=48 * 1024 * 1024
        ),
    )(
        features, theta, section_weight.reshape(1, -1), pair_rows, pair_cols, pair_counts, cotangent
    )
    return outs[0], outs[1], outs[2], outs[3].reshape(-1)


def solution(mesh):
    placed = (
        P("ent", None),
        P(),
        P(("ent", "sec")),
        P(("ent", "sec"), None, None),
        P(("ent", "sec"), None, None),
        P(("ent", "sec"), None),
        P("ent", None),
    )
    return jax.shard_map(
        body,
        mesh=mesh,
        in_specs=placed,
        out_specs=(P("ent", None), P("ent", None), P(), P(("ent", "sec"))),
        check_vma=False,
    )
```

time: 1670 us -> 117 us (0.07)
  the two profiles are of different devices: /device:TPU:0 before, /device:TPU:1 now
where the time goes in v1:
time: 117 us; the launch traced here: 116 us
  Pallas kernels  108 us (92%)
  local copies, waits for them, and re-layouts  8.13 us (7%)
    pallas_call x1, Pallas kernels, body(): pl.pallas_call(layer, out_shape=(jax.ShapeDtypeStruct((128, 256), BF16),...  108 us
    unnamed x18, local copies, waits for them, and re-layouts  8.13 us

profile of v1, /device:TPU:1, one launch (start us, length us, event | category | flops | bytes accessed | tf_op | source)
XLA Modules:
  0.0 116.3 jit_solution(8641401201157594832)
XLA Ops:
  0.6 0.0 copy-start.6
  0.6 0.6 copy-done.6
  1.3 0.0 copy-start
  1.3 0.9 copy-done
  2.2 0.0 copy-start.1
  2.2 0.8 copy-done.1
  3.0 0.0 copy-start.2
  3.0 0.8 copy-done.2
  3.9 0.0 copy-start.3
  3.9 0.8 copy-done.3
  4.7 0.0 copy-start.4
  4.7 0.8 copy-done.4
  5.6 0.0 copy-start.5
  5.6 0.7 copy-done.5
  6.2 107.5 %shard_map.102 = (bf16[128,256]{1,0:T(8,128)(2,1)S(1)}, bf16[128,256]{1,0:T(8,128)(2,1)S(1)}, f32[256,256]{1,0:T(8,128)S(1)}, f32[1,512]{1,0:T(1,128)S(1)}) custom-call(bf16[128,256]{1,0:T(8,128)(2,1)S(1)} %copy-done.1, bf16[256,256]{1,0:T(8,128)(2,1)S(1)} %copy-done, f32[1,512]{1,0:T(1,128)S(1)} %bitcast.2, s32[1,32,512]{2,1,0:T(8,128)S(1)} %copy-done.2, ...), custom_call_target="tpu_custom_call" | custom-call | tf_op jit(solution)/shard_map/pallas_call | solution.py:394
  113.7 0.6 copy.15
  114.4 0.6 copy.16
  115.0 0.7 copy.17
  115.7 0.6 copy.18
Async XLA Ops:
  0.6 0.7 copy-start.6
  1.3 0.9 copy-start
  2.2 0.8 copy-start.1
  3.0 0.8 copy-start.2
  3.9 0.8 copy-start.3
  4.7 0.8 copy-start.4
  5.6 0.7 copy-start.5

commit v2 on v1

v2 whole, which is shorter than its diff:
```python
import jax
import jax.numpy as jnp
from jax import lax
from jax.experimental import pallas as pl
from jax.experimental.pallas import tpu as pltpu
from jax.sharding import PartitionSpec as P

F32 = jnp.float32
BF16 = jnp.bfloat16
MESH = pl.DeviceIdType.MESH
NT = (((1,), (1,)), ((), ()))
NN = (((1,), (0,)), ((), ()))
N_SEM = 200


def dot(a, b, dims):
    return lax.dot_general(a, b, dims, preferred_element_type=F32)


def split(v):
    hi = v.astype(BF16)
    return hi, (v - hi.astype(F32)).astype(BF16)


def layer(
    feat_h, theta_h, sw_h, rows_h, cols_h, counts_h, cot_h,
    act_o, gf_o, gt_o, gw_o,
    feat, theta, rows, cols, counts, cot,
    HT, HS, DS, DR, D1, DX, D2, DP, DW, DT, SW, INV, XF, XT, G, GR, GH, GL, GATH, MT, PF, PB,
    RB, ACC, YS, YR, A2, XR, AS, AR, FS, FR, TH,
    T0, TP, TX, T3, TS, ssem, rsem, lsem,
):
    e = lax.axis_index("ent")
    s = lax.axis_index("sec")
    core = lax.rem(s, 2)
    xl = lax.div(s, 2)
    xh = lax.div(e, 16)
    z = lax.rem(lax.div(e, 4), 4)
    y = lax.rem(e, 4)
    myx = xh * 2 + xl
    half = pl.multiple_of(core * 64, 64)
    other_half = pl.multiple_of((1 - core) * 64, 64)

    loads = [
        pltpu.make_async_copy(src, dst, lsem.at[i])
        for i, (src, dst) in enumerate([
            (feat_h, feat), (cols_h.at[0], cols), (counts_h, counts), (rows_h.at[0], rows),
            (sw_h, SW.at[0]), (theta_h, theta), (cot_h, cot),
        ])
    ]
    for copy in loads:
        copy.start()

    def dev(xh_, xl_, z_, y_):
        return (xh_ * 16 + z_ * 4 + y_, xl_ * 2 + core)

    def mod4(v):
        return lax.rem(v + 4, 4)

    sib = (e, xl * 2 + 1 - core)
    x_pair = dev(1 - xh, 1 - xl, z, y)
    x_far = dev(1 - xh, xl, z, y)
    x_same = dev(xh, 1 - xl, z, y)

    def z_dev(d):
        return dev(xh, xl, mod4(z + d), y)

    def y_dev(d):
        return dev(xh, xl, z, mod4(y + d))

    plane = [(a, b) for a in range(4) for b in range(4) if a or b]
    plane_dev = [dev(xh, xl, mod4(z + a), mod4(y + b)) for a, b in plane]
    pair_z = [dev(1 - xh, 1 - xl, mod4(z + d), y) for d in range(4)]
    pair_y = [dev(1 - xh, 1 - xl, z, mod4(y + d)) for d in range(4)]
    peers = [sib, x_pair, x_far, x_same] + plane_dev + pair_z[1:] + pair_y[1:]
    sent = []

    def send(src, dst, device):
        i = len(sent)
        copy = pltpu.make_async_remote_copy(
            src_ref=src, dst_ref=dst, send_sem=ssem.at[i], recv_sem=rsem.at[i],
            device_id=device, device_id_type=MESH,
        )
        copy.start()
        sent.append(copy)
        return copy

    def arrived(copies):
        for copy in copies:
            copy.wait_recv()

    barrier = pltpu.get_barrier_semaphore()
    for peer in peers:
        pl.semaphore_signal(barrier, inc=1, device_id=peer, device_id_type=MESH)

    slot_row = lax.broadcasted_iota(jnp.int32, (1, 512), 1)
    ent_iota = lax.broadcasted_iota(jnp.int32, (128, 512), 0)

    def col_table(j):
        live = slot_row < counts[0, j]
        col = jnp.where(live, cols[pl.ds(j, 1), :], -1)
        return jnp.where(ent_iota == col, 1.0, 0.0).astype(BF16)

    loads[0].wait()
    for p in range(2):
        XF[0, p, xh, z, y] = feat[pl.ds(pl.multiple_of(half + 32 * p, 32), 32), :]

    pl.semaphore_wait(barrier, len(peers))

    def all_gather(ph, p, lines=None):
        buf = XF.at[ph, p]
        near_dev, pair_dev, ring_dev = (y_dev, pair_y, z_dev) if p == 0 else (z_dev, pair_z, y_dev)

        def line(a):
            return buf.at[a, z] if p == 0 else buf.at[a, :, y]

        own = buf.at[xh, z, y]
        same = [send(own, own, near_dev(d)) for d in (1, 3, 2)]
        pair = [send(own, own, pair_dev[d]) for d in (0, 1, 3, 2)]
        yield
        arrived(same)
        first = [send(line(xh), line(xh), ring_dev(d)) for d in (1, 3, 2)]
        yield
        arrived(pair)
        second = [send(line(1 - xh), line(1 - xh), ring_dev(d)) for d in (1, 3, 2)]
        yield
        for i in range(3):
            arrived([first[i], second[i]])
            yield

    def degree_sum():
        m = [send(DS, DR, sib)]
        yield
        arrived(m)
        v = DS[...] + DR[...]
        v = jnp.where(core == 0, v[:, 0:64], v[:, 64:128])
        D1[...] = jnp.concatenate([v[0:16], v[16:32]], axis=1)
        m = [send(D1, DX.at[i], d) for i, d in enumerate((x_pair, x_same, x_far))]
        yield
        arrived(m)
        D2[...] = D1[...] + DX[0] + DX[1] + DX[2]
        m = [send(D2, DP.at[i], d) for i, d in enumerate(plane_dev)]
        yield
        arrived(m)
        v = D2[...]
        for i in range(15):
            v = v + DP[i]
        DW[...] = jnp.zeros((128, 128), F32)
        DW[0:16, :] = lax.rsqrt(1.0 + v)
        DT[...] = DW[...].T
        yield

    def step(gens):
        for g in gens:
            next(g, None)

    gathers = [all_gather(0, 0), all_gather(0, 1)]
    step(gathers)
    for copy in loads[1:5]:
        copy.wait()
    ones = jnp.ones((8, 512), BF16)

    def degree_block(j, carry):
        DS[pl.ds(j, 1), :] = dot(ones, col_table(j), NT)[0:1]
        return carry

    lax.fori_loop(0, 32, degree_block, 0)
    degrees = degree_sum()
    step([degrees])
    sw_copy = send(SW.at[0], SW.at[1], sib)

    sec_iota = lax.broadcasted_iota(jnp.int32, (512, 512), 0)

    table_copies = []

    def table_line(k):
        a, b = k // 4, k % 4

        def table_block(i, carry):
            j = 4 * k + i
            row_hot = jnp.where(sec_iota == rows[pl.ds(j, 1), :], 1.0, 0.0).astype(BF16)
            block = dot(col_table(j), row_hot, NT).astype(BF16)
            for h in range(2):
                for p in range(2):
                    HT[h, p, a, b, i] = block[h * 64 + p * 32:h * 64 + p * 32 + 32]
            return carry

        lax.fori_loop(0, 4, table_block, 0)
        table_copies.append(send(HT.at[1 - core, :, a, b], HS.at[:, a, b], sib))

    table_line(0)
    step([degrees])
    table_line(1)
    step(gathers)
    table_line(2)
    step(gathers)
    table_line(3)
    step([degrees])
    for k in range(4, 8):
        table_line(k)
    for copy in loads[5:]:
        copy.wait()
    TH[...] = theta[...].T
    for _ in range(3):
        step(gathers)
    arrived(table_copies)
    arrived([sw_copy])
    step([degrees])
    cols_of = [DT[0:64, 0:16], DT[64:128, 0:16]]

    def scale_of(j, p):
        return cols_of[j // 16][p * 32:p * 32 + 32, j % 16:j % 16 + 1]

    own_table = jnp.where(xh == 0, cols_of[0], cols_of[1])
    own_lane = lax.broadcasted_iota(jnp.int32, (64, 16), 1) == z * 4 + y
    own_scale = jnp.sum(jnp.where(own_lane, own_table, 0.0), axis=1, keepdims=True)

    def table_rows(p, i, k):
        ref = HT.at[core, p] if k == 0 else HS.at[p]
        pieces = [(ref[a, i] if p == 0 else ref[a, :, i]).reshape(128, 512) for a in range(2)]
        return jnp.concatenate(pieces, axis=0)

    def core_sum(ph, k, width):
        return send(G.at[ph, k, 0:width], GR.at[ph, k, 0:width], sib)

    def scaled_line(p, i):
        pieces = []
        for a in range(2):
            for o in range(4):
                b, c = (i, o) if p == 0 else (o, i)
                v = XF[0, p, a, b, c].astype(F32) * scale_of(a * 16 + b * 4 + c, p)
                pieces.append(v.astype(BF16))
        return jnp.concatenate(pieces, axis=0)

    for p in range(2):
        for i in range(4):
            XT[p, i, 0:256] = scaled_line(p, i).T
            XT[p, i, 256:272] = jnp.ones((16, 256), BF16)

    exchange = {}
    for k in (1, 0):
        for p in range(2):

            def gather_line(i, carry):
                v = dot(XT[p, i], table_rows(p, i, k), NN)
                G[0, k] += v
                return carry

            if p == 0:
                G[0, k] = jnp.zeros((272, 512), F32)
            lax.fori_loop(0, 4, gather_line, 0)
        exchange[k] = core_sum(0, k, 272)
    for k in (0, 1):
        arrived([exchange[1 - k]])
        g = G[0, k] + GR[0, 1 - k]
        inverse = 1.0 / (1.0 + g[256:257])
        INV[k] = inverse
        hi, lo = split(g[0:256])
        GH[k] = hi
        GL[k] = lo
        gathered = dot(TH[...], hi, NN) + dot(TH[...], lo, NN)
        if k == 0:
            GATH[...] = gathered
        MT[0, k] = ((SW[k] * inverse) * gathered).astype(BF16)

    def reduce_scatter(ph, out):
        rings = [(z_dev, y_dev, z, y), (y_dev, z_dev, y, z)]

        def term(p, i):
            return dot(table_rows(p, i, 0), MT[ph, 0], NT) + dot(table_rows(p, i, 1), MT[ph, 1], NT)

        ring_copies = [[], []]
        for m, d in enumerate((2, 1, 3)):
            for p in range(2):
                ring_dev, _, ring, _ = rings[p]
                PB[ph, p, m] = term(p, mod4(ring + d)).astype(BF16).reshape(2, 4, 32, 256)
                ring_copies[p].append(send(PB.at[ph, p, m], RB.at[ph, p, m], ring_dev(d)))
        for p in range(2):
            PF[p] = term(p, rings[p][2]).reshape(2, 4, 32, 256)
        yield
        axis_copies = [[], []]
        for p in range(2):
            _, axis_dev, _, axis = rings[p]
            arrived(ring_copies[p])
            for o in range(4):
                for a in range(2):
                    v = PF[p, a, o]
                    for m in range(3):
                        v = v + RB[ph, p, m, a, o].astype(F32)
                    ACC[p, o, a] = v
                    YS[ph, p, o, a] = v.astype(BF16)
            for d in (2, 1, 3):
                axis_copies[p].append(send(YS.at[ph, p, mod4(axis + d)], YR.at[ph, p, d - 1], axis_dev(d)))
        yield
        x_copies = [[], []]
        for p in range(2):
            axis = rings[p][3]
            arrived(axis_copies[p])
            for a in range(2):
                v = ACC[p, axis, a]
                for i in range(3):
                    v = v + YR[ph, p, i, a].astype(F32)
                A2[ph, p, a] = v
            x_copies[p] = [
                send(A2.at[ph, p, 1 - xh], XR.at[ph, p, myx], x_far),
                send(A2.at[ph, p, 1 - xh], XR.at[ph, p, myx], x_pair),
                send(A2.at[ph, p, xh], XR.at[ph, p, myx], x_same),
            ]
            XR[ph, p, myx] = A2[ph, p, xh]
        yield
        for p in range(2):
            arrived(x_copies[p])
            out[p] = (XR[ph, p, 0] + XR[ph, p, 1]) + (XR[ph, p, 2] + XR[ph, p, 3])
            yield

    collected = {}
    flow = reduce_scatter(0, collected)
    for _ in range(3):
        next(flow)
    back = []
    for p in range(2):
        next(flow)
        part = slice(p * 32, p * 32 + 32)
        preact = own_scale[part] * collected[p]
        sig = 1.0 / (1.0 + jnp.exp(-preact))
        AS[part, :] = (preact * sig).astype(BF16)
        upstream = cot[pl.ds(pl.multiple_of(half + p * 32, 32), 32), :].astype(F32)
        grad = upstream * sig * (1.0 + preact * (1.0 - sig))
        XF[1, p, xh, z, y] = (own_scale[part] * grad).astype(BF16)
        back.append(all_gather(1, p))
        step([back[p]])
    act_copy = send(AS, AR, sib)
    for k in range(2):
        G[1, k, 0:256] = jnp.zeros((256, 512), F32)

    def back_line(p, i):
        pieces = [(XF[1, p, a, i] if p == 0 else XF[1, p, a, :, i]).reshape(128, 256) for a in range(2)]
        return jnp.concatenate(pieces, axis=0).T

    step(back)
    step(back)
    for k in range(2):
        G[1, k, 0:256] += dot(back_line(0, z), table_rows(0, z, k), NN)
        G[1, k, 0:256] += dot(back_line(1, y), table_rows(1, y, k), NN)
    act_o[pl.ds(half, 64), :] = AS[...]
    arrived([act_copy])
    act_o[pl.ds(other_half, 64), :] = AR[...]
    for d in (3, 1):
        step(back)
        for p, i in enumerate((mod4(z + d), mod4(y + d))):
            xt = back_line(p, i)
            for k in range(2):
                G[1, k, 0:256] += dot(xt, table_rows(p, i, k), NN)
    step(back)
    last = [(0, mod4(z + 2)), (1, mod4(y + 2))]
    last_xt = [back_line(p, i) for p, i in last]
    for k in (1, 0):
        v = G[1, k, 0:256]
        for (p, i), xt in zip(last, last_xt):
            v = v + dot(xt, table_rows(p, i, k), NN)
        G[1, k, 0:256] = v
        exchange[k] = core_sum(1, k, 256)
    for k in (0, 1):
        arrived([exchange[1 - k]])
        g = G[1, k, 0:256] + GR[1, 1 - k, 0:256]
        if k == 0:
            gw_o[...] = jnp.sum(GATH[...] * g, axis=0, keepdims=True) * INV[0]
        MT[1, k] = ((SW[k] * INV[k]) * g).astype(BF16)

    mine = pl.ds(pl.multiple_of(core * 128, 128), 128)
    theirs = pl.ds(pl.multiple_of((1 - core) * 128, 128), 128)
    v = jnp.zeros((128, 256), F32)
    for k in range(2):
        v = v + dot(GH[k, mine, :], MT[1, k], NT) + dot(GL[k, mine, :], MT[1, k], NT)
    T0[...] = v.reshape(4, 4, 8, 256)
    theta_copies = [
        send(T0.at[mod4(z + a), mod4(y + b)], TP.at[i], plane_dev[i]) for i, (a, b) in enumerate(plane)
    ]
    collected = {}
    flow = reduce_scatter(1, collected)
    next(flow)
    arrived(theta_copies)
    v = T0[z, y]
    for i in range(15):
        v = v + TP[i]
    TX[myx] = v
    theta_copies = [send(TX.at[myx], TX.at[myx], d) for d in (x_far, x_pair, x_same)]
    next(flow)
    arrived(theta_copies)
    T3[z, y] = (TX[0] + TX[1]) + (TX[2] + TX[3])
    theta_copies = [send(T3.at[z, y], T3.at[z, y], d) for d in plane_dev]
    next(flow)
    arrived(theta_copies)
    theta_copies = [send(T3, TS, sib)]
    gt_o[mine, :] = T3[...].reshape(128, 256)
    arrived(theta_copies)
    gt_o[theirs, :] = TS[...].reshape(128, 256)
    for p in range(2):
        next(flow)
        part = slice(p * 32, p * 32 + 32)
        hi, lo = split(own_scale[part] * collected[p])
        FS[part, :] = (dot(hi, theta[...], NT) + dot(lo, theta[...], NT)).astype(BF16)
    grad_copy = send(FS, FR, sib)
    gf_o[pl.ds(half, 64), :] = FS[...]
    arrived([grad_copy])
    gf_o[pl.ds(other_half, 64), :] = FR[...]
    assert len(sent) <= N_SEM
    for copy in sent:
        copy.wait_send()


def body(features, theta, section_weight, pair_rows, pair_cols, pair_counts, cotangent):
    vmem = pl.BlockSpec(memory_space=pltpu.VMEM)
    hbm = pl.BlockSpec(memory_space=pltpu.HBM)

    def buf(shape, dtype):
        return pltpu.VMEM(shape, dtype)

    outs = pl.pallas_call(
        layer,
        out_shape=(
            jax.ShapeDtypeStruct((128, 256), BF16),
            jax.ShapeDtypeStruct((128, 256), BF16),
            jax.ShapeDtypeStruct((256, 256), F32),
            jax.ShapeDtypeStruct((1, 512), F32),
        ),
        in_specs=[hbm] * 7,
        out_specs=(vmem, vmem, vmem, vmem),
        scratch_shapes=[
            buf((128, 256), BF16),
            buf((256, 256), BF16),
            buf((32, 512), jnp.int32),
            buf((32, 512), jnp.int32),
            pltpu.SMEM((1, 32), jnp.int32),
            buf((128, 256), BF16),
            buf((2, 2, 2, 4, 4, 32, 512), BF16),
            buf((2, 2, 4, 4, 32, 512), BF16),
            buf((32, 128), F32),
            buf((32, 128), F32),
            buf((16, 128), F32),
            buf((3, 16, 128), F32),
            buf((16, 128), F32),
            buf((15, 16, 128), F32),
            buf((128, 128), F32),
            buf((128, 128), F32),
            buf((2, 1, 512), F32),
            buf((2, 1, 512), F32),
            buf((2, 2, 2, 4, 4, 32, 256), BF16),
            buf((2, 4, 272, 256), BF16),
            buf((2, 2, 272, 512), F32),
            buf((2, 2, 272, 512), F32),
            buf((2, 256, 512), BF16),
            buf((2, 256, 512), BF16),
            buf((256, 512), F32),
            buf((2, 2, 256, 512), BF16),
            buf((2, 2, 4, 32, 256), F32),
            buf((2, 2, 3, 2, 4, 32, 256), BF16),
            buf((2, 2, 3, 2, 4, 32, 256), BF16),
            buf((2, 4, 2, 32, 256), F32),
            buf((2, 2, 4, 2, 32, 256), BF16),
            buf((2, 2, 3, 2, 32, 256), BF16),
            buf((2, 2, 2, 32, 256), F32),
            buf((2, 2, 4, 32, 256), F32),
            buf((64, 256), BF16),
            buf((64, 256), BF16),
            buf((64, 256), BF16),
            buf((64, 256), BF16),
            buf((256, 256), BF16),
            buf((4, 4, 8, 256), F32),
            buf((15, 8, 256), F32),
            buf((4, 8, 256), F32),
            buf((4, 4, 8, 256), F32),
            buf((4, 4, 8, 256), F32),
            pltpu.SemaphoreType.DMA((N_SEM,)),
            pltpu.SemaphoreType.DMA((N_SEM,)),
            pltpu.SemaphoreType.DMA((7,)),
        ],
        compiler_params=pltpu.CompilerParams(
            collective_id=0, has_side_effects=True, vmem_limit_bytes=56 * 1024 * 1024
        ),
    )(
        features, theta, section_weight.reshape(1, -1), pair_rows, pair_cols, pair_counts, cotangent
    )
    return outs[0], outs[1], outs[2], outs[3].reshape(-1)


def solution(mesh):
    placed = (
        P("ent", None),
        P(),
        P(("ent", "sec")),
        P(("ent", "sec"), None, None),
        P(("ent", "sec"), None, None),
        P(("ent", "sec"), None),
        P("ent", None),
    )
    return jax.shard_map(
        body,
        mesh=mesh,
        in_specs=placed,
        out_specs=(P("ent", None), P("ent", None), P(), P(("ent", "sec"))),
        check_vma=False,
    )
```

time: 117 us -> 93.9 us (0.80)
  Pallas kernels: 108 us -> 88.8 us
  local copies, waits for them, and re-layouts: 8.13 us -> 4.28 us
    pallas_call x1, Pallas kernels: 108 us -> 88.8 us  [body(): pl.pallas_call(layer, out_shape=(jax.ShapeDtypeStruct((128, 256), BF16),...]
    unnamed x18 -> x8, local copies, waits for them, and re-layouts: 8.13 us -> 4.28 us
where the time goes in v2:
time: 93.9 us; the launch traced here: 93.7 us
  Pallas kernels  88.8 us (95%)
  local copies, waits for them, and re-layouts  4.28 us (5%)
    pallas_call x1, Pallas kernels, body(): pl.pallas_call(layer, out_shape=(jax.ShapeDtypeStruct((128, 256), BF16),...  88.8 us
    unnamed x8, local copies, waits for them, and re-layouts  4.28 us

profile of v2, /device:TPU:1, one launch (start us, length us, event | category | flops | bytes accessed | tf_op | source)
XLA Modules:
  0.0 93.7 jit_solution(9537979987400423828)
XLA Ops:
  0.6 88.8 %shard_map.102 = (bf16[128,256]{1,0:T(8,128)(2,1)}, bf16[128,256]{1,0:T(8,128)(2,1)}, f32[256,256]{1,0:T(8,128)}, f32[1,512]{1,0:T(1,128)}) custom-call(bf16[128,256]{1,0:T(8,128)(2,1)} %feat_h.1, bf16[256,256]{1,0:T(8,128)(2,1)} %theta_h.1, f32[1,512]{1,0:T(1,128)} %bitcast.2, s32[1,32,512]{2,1,0:T(8,128)} %rows_h.1, s32[1,32,512]{2,1,0:T(8,128)} %cols_h.1, ...), custom_call_target="tpu_custom_call" | custom-call | tf_op jit(solution)/shard_map/pallas_call | solution.py:419
  89.4 0.0 copy-start
  89.4 1.5 %copy.15 = bf16[128,256]{1,0:T(8,128)(2,1)} copy(bf16[128,256]{1,0:T(8,128)(2,1)} %get-tuple-element.16) | data formatting | bytes 131072
  90.9 1.5 %copy.16 = bf16[128,256]{1,0:T(8,128)(2,1)} copy(bf16[128,256]{1,0:T(8,128)(2,1)} %get-tuple-element.17) | data formatting | bytes 131072
  92.4 0.0 copy-done
  92.4 0.0 copy-start.1
  92.4 0.7 copy.17
  93.1 0.0 copy-done.1
  93.1 0.6 copy.18
Async XLA Ops:
  89.4 3.0 %copy-start = (f32[256,256]{1,0:T(8,128)S(1)}, f32[256,256]{1,0:T(8,128)}, u32[]{:S(2)}) copy-start(f32[256,256]{1,0:T(8,128)} %get-tuple-element.18) | copy-start | bytes 786436
  92.4 0.7 copy-start.1

commit v3 on v2

--- a/solution.py
+++ b/solution.py
@@ -26,7 +26,7 @@
     feat_h, theta_h, sw_h, rows_h, cols_h, counts_h, cot_h,
     act_o, gf_o, gt_o, gw_o,
     feat, theta, rows, cols, counts, cot,
-    HT, HS, DS, DR, D1, DX, D2, DP, DW, DT, SW, INV, XF, XT, G, GR, GH, GL, GATH, MT, PF, PB,
+    HT, HS, DS, DR, D1, DX, D2, DP, DW, DT, SW, INV, XF, SC, G, GR, GH, GL, GATH, MT, PF, PB,
     RB, ACC, YS, YR, A2, XR, AS, AR, FS, FR, TH,
     T0, TP, TX, T3, TS, ssem, rsem, lsem,
 ):
@@ -101,6 +101,13 @@
         col = jnp.where(live, cols[pl.ds(j, 1), :], -1)
         return jnp.where(ent_iota == col, 1.0, 0.0).astype(BF16)
 
+    for copy in loads[1:3]:
+        copy.wait()
+    ones = jnp.ones((8, 512), BF16)
+    for k in range(8):
+        table = jnp.concatenate([col_table(4 * k + i) for i in range(4)], axis=0)
+        DS[k:k + 1, :] = dot(ones, table, NT)[0:1]
+
     loads[0].wait()
     for p in range(2):
         XF[0, p, xh, z, y] = feat[pl.ds(pl.multiple_of(half + 32 * p, 32), 32), :]
@@ -133,6 +140,7 @@
         yield
         arrived(m)
         v = DS[...] + DR[...]
+        v = jnp.concatenate([v[:, i * 128:(i + 1) * 128] for i in range(4)], axis=0)
         v = jnp.where(core == 0, v[:, 0:64], v[:, 64:128])
         D1[...] = jnp.concatenate([v[0:16], v[16:32]], axis=1)
         m = [send(D1, DX.at[i], d) for i, d in enumerate((x_pair, x_same, x_far))]
@@ -154,20 +162,11 @@
         for g in gens:
             next(g, None)
 
+    degrees = degree_sum()
+    step([degrees])
     gathers = [all_gather(0, 0), all_gather(0, 1)]
     step(gathers)
-    for copy in loads[1:5]:
-        copy.wait()
-    ones = jnp.ones((8, 512), BF16)
-
-    def degree_block(j, carry):
-        DS[pl.ds(j, 1), :] = dot(ones, col_table(j), NT)[0:1]
-        return carry
-
-    lax.fori_loop(0, 32, degree_block, 0)
-    degrees = degree_sum()
-    step([degrees])
-    sw_copy = send(SW.at[0], SW.at[1], sib)
+    loads[3].wait()
 
     sec_iota = lax.broadcasted_iota(jnp.int32, (512, 512), 0)
 
@@ -188,32 +187,31 @@
         lax.fori_loop(0, 4, table_block, 0)
         table_copies.append(send(HT.at[1 - core, :, a, b], HS.at[:, a, b], sib))
 
-    table_line(0)
     step([degrees])
-    table_line(1)
+    for k in range(3):
+        table_line(k)
+    step([degrees])
     step(gathers)
-    table_line(2)
     step(gathers)
-    table_line(3)
-    step([degrees])
-    for k in range(4, 8):
+    loads[4].wait()
+    sw_copy = send(SW.at[0], SW.at[1], sib)
+    for k in range(3, 8):
         table_line(k)
     for copy in loads[5:]:
         copy.wait()
     TH[...] = theta[...].T
-    for _ in range(3):
-        step(gathers)
-    arrived(table_copies)
-    arrived([sw_copy])
     step([degrees])
     cols_of = [DT[0:64, 0:16], DT[64:128, 0:16]]
-
-    def scale_of(j, p):
-        return cols_of[j // 16][p * 32:p * 32 + 32, j % 16:j % 16 + 1]
-
-    own_table = jnp.where(xh == 0, cols_of[0], cols_of[1])
-    own_lane = lax.broadcasted_iota(jnp.int32, (64, 16), 1) == z * 4 + y
-    own_scale = jnp.sum(jnp.where(own_lane, own_table, 0.0), axis=1, keepdims=True)
+    for c in range(4):
+        for a in range(2):
+            for b in range(4):
+                r = c * 8 + a * 4 + b
+                column = cols_of[r // 16][:, r % 16:r % 16 + 1]
+                for p in range(2):
+                    SC[p, a, b, c] = jnp.broadcast_to(column[p * 32:p * 32 + 32], (32, 128))
+
+    own_scale = jnp.concatenate([SC[p, xh, z, y] for p in range(2)], axis=0)
+    own_scale = jnp.concatenate([own_scale, own_scale], axis=1)
 
     def table_rows(p, i, k):
         ref = HT.at[core, p] if k == 0 else HS.at[p]
@@ -223,33 +221,51 @@
     def core_sum(ph, k, width):
         return send(G.at[ph, k, 0:width], GR.at[ph, k, 0:width], sib)
 
-    def scaled_line(p, i):
+    def line_of(ref, p, a, i):
+        return ref[p, a, i] if p == 0 else ref[p, a, :, i]
+
+    def gather_line(ph, p, i):
         pieces = []
         for a in range(2):
-            for o in range(4):
-                b, c = (i, o) if p == 0 else (o, i)
-                v = XF[0, p, a, b, c].astype(F32) * scale_of(a * 16 + b * 4 + c, p)
-                pieces.append(v.astype(BF16))
-        return jnp.concatenate(pieces, axis=0)
-
-    for p in range(2):
-        for i in range(4):
-            XT[p, i, 0:256] = scaled_line(p, i).T
-            XT[p, i, 256:272] = jnp.ones((16, 256), BF16)
-
-    exchange = {}
-    for k in (1, 0):
-        for p in range(2):
-
-            def gather_line(i, carry):
-                v = dot(XT[p, i], table_rows(p, i, k), NN)
-                G[0, k] += v
-                return carry
-
-            if p == 0:
-                G[0, k] = jnp.zeros((272, 512), F32)
-            lax.fori_loop(0, 4, gather_line, 0)
-        exchange[k] = core_sum(0, k, 272)
+            v = line_of(XF.at[ph], p, a, i).reshape(128, 256)
+            if ph == 0:
+                scale = line_of(SC, p, a, i).reshape(128, 128)
+                v = (v.astype(F32) * jnp.concatenate([scale, scale], axis=1)).astype(BF16)
+            pieces.append(v)
+        xt = jnp.concatenate(pieces, axis=0).T
+        if ph == 0:
+            xt = jnp.concatenate([xt, jnp.ones((16, 256), BF16)], axis=0)
+        return xt
+
+    def gather_sections(ph, gathers):
+        width = 272 if ph == 0 else 256
+        exchange = {}
+        for k in range(2):
+            v = None
+            for p, i in enumerate((z, y)):
+                t = dot(gather_line(ph, p, i), table_rows(p, i, k), NN)
+                v = t if v is None else v + t
+            G[ph, k, 0:width] = v
+        for d in (3, 1):
+            step(gathers)
+            for p, i in enumerate((mod4(z + d), mod4(y + d))):
+                xt = gather_line(ph, p, i)
+                for k in range(2):
+                    G[ph, k, 0:width] += dot(xt, table_rows(p, i, k), NN)
+        step(gathers)
+        last = [(0, mod4(z + 2)), (1, mod4(y + 2))]
+        xts = [gather_line(ph, p, i) for p, i in last]
+        for k in (1, 0):
+            v = G[ph, k, 0:width]
+            for (p, i), xt in zip(last, xts):
+                v = v + dot(xt, table_rows(p, i, k), NN)
+            G[ph, k, 0:width] = v
+            exchange[k] = core_sum(ph, k, width)
+        return exchange
+
+    arrived(table_copies)
+    arrived([sw_copy])
+    exchange = gather_sections(0, gathers)
     for k in (0, 1):
         arrived([exchange[1 - k]])
         g = G[0, k] + GR[0, 1 - k]
@@ -300,7 +316,7 @@
                 v = ACC[p, axis, a]
                 for i in range(3):
                     v = v + YR[ph, p, i, a].astype(F32)
-                A2[ph, p, a] = v
+                A2[ph, p, a] = v.astype(BF16)
             x_copies[p] = [
                 send(A2.at[ph, p, 1 - xh], XR.at[ph, p, myx], x_far),
                 send(A2.at[ph, p, 1 - xh], XR.at[ph, p, myx], x_pair),
@@ -310,13 +326,15 @@
         yield
         for p in range(2):
             arrived(x_copies[p])
-            out[p] = (XR[ph, p, 0] + XR[ph, p, 1]) + (XR[ph, p, 2] + XR[ph, p, 3])
+            terms = [XR[ph, p, i].astype(F32) for i in range(4)]
+            out[p] = (terms[0] + terms[1]) + (terms[2] + terms[3])
             yield
 
     collected = {}
     flow = reduce_scatter(0, collected)
-    for _ in range(3):
-        next(flow)
+    next(flow)
+    next(flow)
+    next(flow)
     back = []
     for p in range(2):
         next(flow)
@@ -330,36 +348,12 @@
         back.append(all_gather(1, p))
         step([back[p]])
     act_copy = send(AS, AR, sib)
-    for k in range(2):
-        G[1, k, 0:256] = jnp.zeros((256, 512), F32)
-
-    def back_line(p, i):
-        pieces = [(XF[1, p, a, i] if p == 0 else XF[1, p, a, :, i]).reshape(128, 256) for a in range(2)]
-        return jnp.concatenate(pieces, axis=0).T
-
     step(back)
     step(back)
-    for k in range(2):
-        G[1, k, 0:256] += dot(back_line(0, z), table_rows(0, z, k), NN)
-        G[1, k, 0:256] += dot(back_line(1, y), table_rows(1, y, k), NN)
     act_o[pl.ds(half, 64), :] = AS[...]
     arrived([act_copy])
     act_o[pl.ds(other_half, 64), :] = AR[...]
-    for d in (3, 1):
-        step(back)
-        for p, i in enumerate((mod4(z + d), mod4(y + d))):
-            xt = back_line(p, i)
-            for k in range(2):
-                G[1, k, 0:256] += dot(xt, table_rows(p, i, k), NN)
-    step(back)
-    last = [(0, mod4(z + 2)), (1, mod4(y + 2))]
-    last_xt = [back_line(p, i) for p, i in last]
-    for k in (1, 0):
-        v = G[1, k, 0:256]
-        for (p, i), xt in zip(last, last_xt):
-            v = v + dot(xt, table_rows(p, i, k), NN)
-        G[1, k, 0:256] = v
-        exchange[k] = core_sum(1, k, 256)
+    exchange = gather_sections(1, back)
     for k in (0, 1):
         arrived([exchange[1 - k]])
         g = G[1, k, 0:256] + GR[1, 1 - k, 0:256]
@@ -409,6 +403,15 @@
         copy.wait_send()
 
 
+def write_out(a, b, c, d, a_o, b_o, c_o, d_o, sem):
+    pairs = [(a, a_o), (b, b_o), (c, c_o), (d, d_o)]
+    copies = [pltpu.make_async_copy(src, dst, sem.at[i]) for i, (src, dst) in enumerate(pairs)]
+    for copy in copies:
+        copy.start()
+    for copy in copies:
+        copy.wait()
+
+
 def body(features, theta, section_weight, pair_rows, pair_cols, pair_counts, cotangent):
     vmem = pl.BlockSpec(memory_space=pltpu.VMEM)
     hbm = pl.BlockSpec(memory_space=pltpu.HBM)
@@ -416,6 +419,8 @@
     def buf(shape, dtype):
         return pltpu.VMEM(shape, dtype)
 
+    ins = (features, theta, section_weight.reshape(1, -1), pair_rows, pair_cols, pair_counts, cotangent)
+    ins = [pltpu.with_memory_space_constraint(v, pltpu.HBM) for v in ins]
     outs = pl.pallas_call(
         layer,
         out_shape=(
@@ -435,8 +440,8 @@
             buf((128, 256), BF16),
             buf((2, 2, 2, 4, 4, 32, 512), BF16),
             buf((2, 2, 4, 4, 32, 512), BF16),
-            buf((32, 128), F32),
-            buf((32, 128), F32),
+            buf((8, 512), F32),
+            buf((8, 512), F32),
             buf((16, 128), F32),
             buf((3, 16, 128), F32),
             buf((16, 128), F32),
@@ -446,7 +451,7 @@
             buf((2, 1, 512), F32),
             buf((2, 1, 512), F32),
             buf((2, 2, 2, 4, 4, 32, 256), BF16),
-            buf((2, 4, 272, 256), BF16),
+            buf((2, 2, 4, 4, 32, 128), F32),
             buf((2, 2, 272, 512), F32),
             buf((2, 2, 272, 512), F32),
             buf((2, 256, 512), BF16),
@@ -459,8 +464,8 @@
             buf((2, 4, 2, 32, 256), F32),
             buf((2, 2, 4, 2, 32, 256), BF16),
             buf((2, 2, 3, 2, 32, 256), BF16),
-            buf((2, 2, 2, 32, 256), F32),
-            buf((2, 2, 4, 32, 256), F32),
+            buf((2, 2, 2, 32, 256), BF16),
+            buf((2, 2, 4, 32, 256), BF16),
             buf((64, 256), BF16),
             buf((64, 256), BF16),
             buf((64, 256), BF16),
@@ -476,11 +481,18 @@
             pltpu.SemaphoreType.DMA((7,)),
         ],
         compiler_params=pltpu.CompilerParams(
-            collective_id=0, has_side_effects=True, vmem_limit_bytes=56 * 1024 * 1024
+            collective_id=0, has_side_effects=True, vmem_limit_bytes=40 * 1024 * 1024
         ),
-    )(
-        features, theta, section_weight.reshape(1, -1), pair_rows, pair_cols, pair_counts, cotangent
-    )
+    )(*ins)
+    anywhere = pl.BlockSpec(memory_space=pl.ANY)
+    outs = pl.pallas_call(
+        write_out,
+        out_shape=tuple(jax.ShapeDtypeStruct(o.shape, o.dtype) for o in outs),
+        in_specs=[vmem] * 4,
+        out_specs=(anywhere,) * 4,
+        scratch_shapes=[pltpu.SemaphoreType.DMA((4,))],
+        compiler_params=pltpu.CompilerParams(vmem_limit_bytes=4 * 1024 * 1024),
+    )(*outs)
     return outs[0], outs[1], outs[2], outs[3].reshape(-1)
 
 

time: 93.9 us -> 81.4 us (0.87)
  Pallas kernels: 88.8 us -> 80.6 us
  local copies, waits for them, and re-layouts: 4.28 us -> 0 us
    pallas_call x1, Pallas kernels: 88.8 us -> 79.8 us  [body(): pl.pallas_call(layer, out_shape=(jax.ShapeDtypeStruct((128, 256), BF16),...]
    unnamed x8 -> x0, local copies, waits for them, and re-layouts: 4.28 us -> none
where the time goes in v3:
time: 81.4 us; the launch traced here: 81.3 us
  Pallas kernels  80.6 us (99%)
    pallas_call x1, Pallas kernels, body(): pl.pallas_call(layer, out_shape=(jax.ShapeDtypeStruct((128, 256), BF16),...  79.8 us

profile of v3, /device:TPU:1, one launch (start us, length us, event | category | flops | bytes accessed | tf_op | source)
XLA Modules:
  0.0 81.3 jit_solution(6631050847421207227)
XLA Ops:
  0.6 79.8 %shard_map.102 = (bf16[128,256]{1,0:T(8,128)(2,1)S(1)}, bf16[128,256]{1,0:T(8,128)(2,1)S(1)}, f32[256,256]{1,0:T(8,128)S(1)}, f32[1,512]{1,0:T(1,128)S(1)}) custom-call(bf16[128,256]{1,0:T(8,128)(2,1)} %feat_h.1, bf16[256,256]{1,0:T(8,128)(2,1)} %theta_h.1, f32[1,512]{1,0:T(1,128)} %bitcast.2, s32[1,32,512]{2,1,0:T(8,128)} %rows_h.1, s32[1,32,512]{2,1,0:T(8,128)} %cols_h.1, ...), custom_call_target="tpu_custom_call" | custom-call | tf_op jit(solution)/shard_map/pallas_call | solution.py:424
  80.5 0.8 shard_map.103

commit v4 on v3

--- a/solution.py
+++ b/solution.py
@@ -7,10 +7,11 @@
 
 F32 = jnp.float32
 BF16 = jnp.bfloat16
+F8 = jnp.float8_e4m3fn
 MESH = pl.DeviceIdType.MESH
 NT = (((1,), (1,)), ((), ()))
 NN = (((1,), (0,)), ((), ()))
-N_SEM = 200
+N_SEM = 48
 
 
 def dot(a, b, dims):
@@ -26,7 +27,7 @@
     feat_h, theta_h, sw_h, rows_h, cols_h, counts_h, cot_h,
     act_o, gf_o, gt_o, gw_o,
     feat, theta, rows, cols, counts, cot,
-    HT, HS, DS, DR, D1, DX, D2, DP, DW, DT, SW, INV, XF, SC, G, GR, GH, GL, GATH, MT, PF, PB,
+    HT, HS, DS, DR, D1, DX, D2, DP, DW, DT, SW, INV, XF, SC, G, GR, LF, LB, LR, GH, GL, GATH, MT, PF, PB,
     RB, ACC, YS, YR, A2, XR, AS, AR, FS, FR, TH,
     T0, TP, TX, T3, TS, ssem, rsem, lsem,
 ):
@@ -73,21 +74,32 @@
     pair_z = [dev(1 - xh, 1 - xl, mod4(z + d), y) for d in range(4)]
     pair_y = [dev(1 - xh, 1 - xl, z, mod4(y + d)) for d in range(4)]
     peers = [sib, x_pair, x_far, x_same] + plane_dev + pair_z[1:] + pair_y[1:]
-    sent = []
-
-    def send(src, dst, device):
-        i = len(sent)
-        copy = pltpu.make_async_remote_copy(
-            src_ref=src, dst_ref=dst, send_sem=ssem.at[i], recv_sem=rsem.at[i],
+    groups = []
+
+    def open_group(size):
+        groups.append(size)
+        return len(groups) - 1
+
+    def send(g, src, dst, device):
+        pltpu.make_async_remote_copy(
+            src_ref=src, dst_ref=dst, send_sem=ssem.at[g], recv_sem=rsem.at[g],
             device_id=device, device_id_type=MESH,
+        ).start()
+
+    def whole(g):
+        return pltpu.make_async_remote_copy(
+            src_ref=groups[g], dst_ref=groups[g], send_sem=ssem.at[g], recv_sem=rsem.at[g],
+            device_id=sib, device_id_type=MESH,
         )
-        copy.start()
-        sent.append(copy)
-        return copy
-
-    def arrived(copies):
-        for copy in copies:
-            copy.wait_recv()
+
+    def send_all(size, copies):
+        g = open_group(size)
+        for src, dst, device in copies:
+            send(g, src, dst, device)
+        return g
+
+    def arrived(g):
+        whole(g).wait_recv()
 
     barrier = pltpu.get_barrier_semaphore()
     for peer in peers:
@@ -99,11 +111,11 @@
     def col_table(j):
         live = slot_row < counts[0, j]
         col = jnp.where(live, cols[pl.ds(j, 1), :], -1)
-        return jnp.where(ent_iota == col, 1.0, 0.0).astype(BF16)
+        return jnp.where(ent_iota == col, 1.0, 0.0).astype(F8)
 
     for copy in loads[1:3]:
         copy.wait()
-    ones = jnp.ones((8, 512), BF16)
+    ones = jnp.ones((8, 512), F8)
     for k in range(8):
         table = jnp.concatenate([col_table(4 * k + i) for i in range(4)], axis=0)
         DS[k:k + 1, :] = dot(ones, table, NT)[0:1]
@@ -122,32 +134,32 @@
             return buf.at[a, z] if p == 0 else buf.at[a, :, y]
 
         own = buf.at[xh, z, y]
-        same = [send(own, own, near_dev(d)) for d in (1, 3, 2)]
-        pair = [send(own, own, pair_dev[d]) for d in (0, 1, 3, 2)]
-        yield
-        arrived(same)
-        first = [send(line(xh), line(xh), ring_dev(d)) for d in (1, 3, 2)]
-        yield
-        arrived(pair)
-        second = [send(line(1 - xh), line(1 - xh), ring_dev(d)) for d in (1, 3, 2)]
-        yield
-        for i in range(3):
-            arrived([first[i], second[i]])
+        same = send_all(buf.at[0, 0, 0:3], [(own, own, near_dev(d)) for d in (1, 3, 2)])
+        pair = send_all(buf.at[0, 0], [(own, own, pair_dev[d]) for d in (0, 1, 3, 2)])
+        rings = {d: open_group(buf.at[0, 0:2]) for d in (1, 3, 2)}
+        yield
+        for stage, a in ((same, xh), (pair, 1 - xh)):
+            arrived(stage)
+            for d in (1, 3, 2):
+                send(rings[d], line(a), line(a), ring_dev(d))
             yield
+        for d in (1, 3, 2):
+            arrived(rings[d])
+            yield
 
     def degree_sum():
-        m = [send(DS, DR, sib)]
+        m = send_all(DR, [(DS, DR, sib)])
         yield
         arrived(m)
         v = DS[...] + DR[...]
         v = jnp.concatenate([v[:, i * 128:(i + 1) * 128] for i in range(4)], axis=0)
         v = jnp.where(core == 0, v[:, 0:64], v[:, 64:128])
         D1[...] = jnp.concatenate([v[0:16], v[16:32]], axis=1)
-        m = [send(D1, DX.at[i], d) for i, d in enumerate((x_pair, x_same, x_far))]
+        m = send_all(DX, [(D1, DX.at[i], d) for i, d in enumerate((x_pair, x_same, x_far))])
         yield
         arrived(m)
         D2[...] = D1[...] + DX[0] + DX[1] + DX[2]
-        m = [send(D2, DP.at[i], d) for i, d in enumerate(plane_dev)]
+        m = send_all(DP, [(D2, DP.at[i], d) for i, d in enumerate(plane_dev)])
         yield
         arrived(m)
         v = D2[...]
@@ -170,14 +182,14 @@
 
     sec_iota = lax.broadcasted_iota(jnp.int32, (512, 512), 0)
 
-    table_copies = []
+    table_group = open_group(HS)
 
     def table_line(k):
         a, b = k // 4, k % 4
 
         def table_block(i, carry):
             j = 4 * k + i
-            row_hot = jnp.where(sec_iota == rows[pl.ds(j, 1), :], 1.0, 0.0).astype(BF16)
+            row_hot = jnp.where(sec_iota == rows[pl.ds(j, 1), :], 1.0, 0.0).astype(F8)
             block = dot(col_table(j), row_hot, NT).astype(BF16)
             for h in range(2):
                 for p in range(2):
@@ -185,7 +197,7 @@
             return carry
 
         lax.fori_loop(0, 4, table_block, 0)
-        table_copies.append(send(HT.at[1 - core, :, a, b], HS.at[:, a, b], sib))
+        send(table_group, HT.at[1 - core, :, a, b], HS.at[:, a, b], sib)
 
     step([degrees])
     for k in range(3):
@@ -194,7 +206,7 @@
     step(gathers)
     step(gathers)
     loads[4].wait()
-    sw_copy = send(SW.at[0], SW.at[1], sib)
+    sw_group = send_all(SW.at[1], [(SW.at[0], SW.at[1], sib)])
     for k in range(3, 8):
         table_line(k)
     for copy in loads[5:]:
@@ -218,8 +230,8 @@
         pieces = [(ref[a, i] if p == 0 else ref[a, :, i]).reshape(128, 512) for a in range(2)]
         return jnp.concatenate(pieces, axis=0)
 
-    def core_sum(ph, k, width):
-        return send(G.at[ph, k, 0:width], GR.at[ph, k, 0:width], sib)
+    def core_sum(src, dst):
+        return send_all(dst, [(src, dst, sib)])
 
     def line_of(ref, p, a, i):
         return ref[p, a, i] if p == 0 else ref[p, a, :, i]
@@ -239,7 +251,7 @@
 
     def gather_sections(ph, gathers):
         width = 272 if ph == 0 else 256
-        exchange = {}
+        exchange = []
         for k in range(2):
             v = None
             for p, i in enumerate((z, y)):
@@ -252,22 +264,30 @@
                 xt = gather_line(ph, p, i)
                 for k in range(2):
                     G[ph, k, 0:width] += dot(xt, table_rows(p, i, k), NN)
+        if ph == 1:
+            exchange.append(send_all(GR.at[1, :, 0:256], [(G.at[1, :, 0:256], GR.at[1, :, 0:256], sib)]))
         step(gathers)
         last = [(0, mod4(z + 2)), (1, mod4(y + 2))]
         xts = [gather_line(ph, p, i) for p, i in last]
         for k in (1, 0):
-            v = G[ph, k, 0:width]
+            v = None
             for (p, i), xt in zip(last, xts):
-                v = v + dot(xt, table_rows(p, i, k), NN)
-            G[ph, k, 0:width] = v
-            exchange[k] = core_sum(ph, k, width)
+                t = dot(xt, table_rows(p, i, k), NN)
+                v = t if v is None else v + t
+            if ph == 0:
+                G[0, k] += v
+                exchange.append(core_sum(G.at[0, k], GR.at[0, k]))
+            else:
+                LF[k] = v
+                LB[k] = v.astype(BF16)
+                exchange.append(core_sum(LB.at[k], LR.at[k]))
         return exchange
 
-    arrived(table_copies)
-    arrived([sw_copy])
+    arrived(table_group)
+    arrived(sw_group)
     exchange = gather_sections(0, gathers)
     for k in (0, 1):
-        arrived([exchange[1 - k]])
+        arrived(exchange[k])
         g = G[0, k] + GR[0, 1 - k]
         inverse = 1.0 / (1.0 + g[256:257])
         INV[k] = inverse
@@ -285,19 +305,19 @@
         def term(p, i):
             return dot(table_rows(p, i, 0), MT[ph, 0], NT) + dot(table_rows(p, i, 1), MT[ph, 1], NT)
 
-        ring_copies = [[], []]
+        ring_groups = [open_group(RB.at[ph, p]) for p in range(2)]
         for m, d in enumerate((2, 1, 3)):
             for p in range(2):
                 ring_dev, _, ring, _ = rings[p]
                 PB[ph, p, m] = term(p, mod4(ring + d)).astype(BF16).reshape(2, 4, 32, 256)
-                ring_copies[p].append(send(PB.at[ph, p, m], RB.at[ph, p, m], ring_dev(d)))
+                send(ring_groups[p], PB.at[ph, p, m], RB.at[ph, p, m], ring_dev(d))
         for p in range(2):
             PF[p] = term(p, rings[p][2]).reshape(2, 4, 32, 256)
         yield
-        axis_copies = [[], []]
+        axis_groups = []
         for p in range(2):
             _, axis_dev, _, axis = rings[p]
-            arrived(ring_copies[p])
+            arrived(ring_groups[p])
             for o in range(4):
                 for a in range(2):
                     v = PF[p, a, o]
@@ -305,27 +325,30 @@
                         v = v + RB[ph, p, m, a, o].astype(F32)
                     ACC[p, o, a] = v
                     YS[ph, p, o, a] = v.astype(BF16)
-            for d in (2, 1, 3):
-                axis_copies[p].append(send(YS.at[ph, p, mod4(axis + d)], YR.at[ph, p, d - 1], axis_dev(d)))
-        yield
-        x_copies = [[], []]
+            axis_groups.append(send_all(
+                YR.at[ph, p],
+                [(YS.at[ph, p, mod4(axis + d)], YR.at[ph, p, d - 1], axis_dev(d)) for d in (2, 1, 3)],
+            ))
+        yield
+        x_groups = []
         for p in range(2):
             axis = rings[p][3]
-            arrived(axis_copies[p])
+            arrived(axis_groups[p])
             for a in range(2):
                 v = ACC[p, axis, a]
                 for i in range(3):
                     v = v + YR[ph, p, i, a].astype(F32)
                 A2[ph, p, a] = v.astype(BF16)
-            x_copies[p] = [
-                send(A2.at[ph, p, 1 - xh], XR.at[ph, p, myx], x_far),
-                send(A2.at[ph, p, 1 - xh], XR.at[ph, p, myx], x_pair),
-                send(A2.at[ph, p, xh], XR.at[ph, p, myx], x_same),
-            ]
+            slot = XR.at[ph, p, myx]
+            x_groups.append(send_all(XR.at[ph, p, 0:3], [
+                (A2.at[ph, p, 1 - xh], slot, x_far),
+                (A2.at[ph, p, 1 - xh], slot, x_pair),
+                (A2.at[ph, p, xh], slot, x_same),
+            ]))
             XR[ph, p, myx] = A2[ph, p, xh]
         yield
         for p in range(2):
-            arrived(x_copies[p])
+            arrived(x_groups[p])
             terms = [XR[ph, p, i].astype(F32) for i in range(4)]
             out[p] = (terms[0] + terms[1]) + (terms[2] + terms[3])
             yield
@@ -347,16 +370,18 @@
         XF[1, p, xh, z, y] = (own_scale[part] * grad).astype(BF16)
         back.append(all_gather(1, p))
         step([back[p]])
-    act_copy = send(AS, AR, sib)
+    act_group = send_all(AR, [(AS, AR, sib)])
     step(back)
     step(back)
     act_o[pl.ds(half, 64), :] = AS[...]
-    arrived([act_copy])
+    arrived(act_group)
     act_o[pl.ds(other_half, 64), :] = AR[...]
     exchange = gather_sections(1, back)
+    arrived(exchange[0])
     for k in (0, 1):
-        arrived([exchange[1 - k]])
-        g = G[1, k, 0:256] + GR[1, 1 - k, 0:256]
+        early = G[1, k, 0:256] + GR[1, 1 - k, 0:256]
+        arrived(exchange[1 + k])
+        g = early + (LF[k] + LR[1 - k].astype(F32))
         if k == 0:
             gw_o[...] = jnp.sum(GATH[...] * g, axis=0, keepdims=True) * INV[0]
         MT[1, k] = ((SW[k] * INV[k]) * g).astype(BF16)
@@ -367,40 +392,41 @@
     for k in range(2):
         v = v + dot(GH[k, mine, :], MT[1, k], NT) + dot(GL[k, mine, :], MT[1, k], NT)
     T0[...] = v.reshape(4, 4, 8, 256)
-    theta_copies = [
-        send(T0.at[mod4(z + a), mod4(y + b)], TP.at[i], plane_dev[i]) for i, (a, b) in enumerate(plane)
-    ]
+    theta_group = send_all(
+        TP,
+        [(T0.at[mod4(z + a), mod4(y + b)], TP.at[i], plane_dev[i]) for i, (a, b) in enumerate(plane)],
+    )
     collected = {}
     flow = reduce_scatter(1, collected)
     next(flow)
-    arrived(theta_copies)
+    arrived(theta_group)
     v = T0[z, y]
     for i in range(15):
         v = v + TP[i]
     TX[myx] = v
-    theta_copies = [send(TX.at[myx], TX.at[myx], d) for d in (x_far, x_pair, x_same)]
+    theta_group = send_all(TX.at[0:3], [(TX.at[myx], TX.at[myx], d) for d in (x_far, x_pair, x_same)])
     next(flow)
-    arrived(theta_copies)
+    arrived(theta_group)
     T3[z, y] = (TX[0] + TX[1]) + (TX[2] + TX[3])
-    theta_copies = [send(T3.at[z, y], T3.at[z, y], d) for d in plane_dev]
+    theta_group = send_all(TP, [(T3.at[z, y], T3.at[z, y], d) for d in plane_dev])
     next(flow)
-    arrived(theta_copies)
-    theta_copies = [send(T3, TS, sib)]
+    arrived(theta_group)
+    theta_group = send_all(TS, [(T3, TS, sib)])
     gt_o[mine, :] = T3[...].reshape(128, 256)
-    arrived(theta_copies)
+    arrived(theta_group)
     gt_o[theirs, :] = TS[...].reshape(128, 256)
     for p in range(2):
         next(flow)
         part = slice(p * 32, p * 32 + 32)
         hi, lo = split(own_scale[part] * collected[p])
         FS[part, :] = (dot(hi, theta[...], NT) + dot(lo, theta[...], NT)).astype(BF16)
-    grad_copy = send(FS, FR, sib)
+    grad_group = send_all(FR, [(FS, FR, sib)])
     gf_o[pl.ds(half, 64), :] = FS[...]
-    arrived([grad_copy])
+    arrived(grad_group)
     gf_o[pl.ds(other_half, 64), :] = FR[...]
-    assert len(sent) <= N_SEM
-    for copy in sent:
-        copy.wait_send()
+    assert len(groups) == N_SEM, len(groups)
+    for g in range(len(groups)):
+        whole(g).wait_send()
 
 
 def write_out(a, b, c, d, a_o, b_o, c_o, d_o, sem):
@@ -454,6 +480,9 @@
             buf((2, 2, 4, 4, 32, 128), F32),
             buf((2, 2, 272, 512), F32),
             buf((2, 2, 272, 512), F32),
+            buf((2, 256, 512), F32),
+            buf((2, 256, 512), BF16),
+            buf((2, 256, 512), BF16),
             buf((2, 256, 512), BF16),
             buf((2, 256, 512), BF16),
             buf((256, 512), F32),

time: 81.4 us -> 78 us (0.958)
  Pallas kernels: 80.6 us -> 77.2 us
    pallas_call x1, Pallas kernels: 79.8 us -> 76.5 us  [body(): pl.pallas_call(layer, out_shape=(jax.ShapeDtypeStruct((128, 256), BF16),...]
where the time goes in v4:
time: 78 us; the launch traced here: 77.9 us
  Pallas kernels  77.2 us (99%)
    pallas_call x1, Pallas kernels, body(): pl.pallas_call(layer, out_shape=(jax.ShapeDtypeStruct((128, 256), BF16),...  76.5 us

profile of v4, /device:TPU:1, one launch (start us, length us, event | category | flops | bytes accessed | tf_op | source)
XLA Modules:
  0.0 77.9 jit_solution(2058318849697005024)
XLA Ops:
  0.6 76.5 %shard_map.102 = (bf16[128,256]{1,0:T(8,128)(2,1)S(1)}, bf16[128,256]{1,0:T(8,128)(2,1)S(1)}, f32[256,256]{1,0:T(8,128)S(1)}, f32[1,512]{1,0:T(1,128)S(1)}) custom-call(bf16[128,256]{1,0:T(8,128)(2,1)} %feat_h.1, bf16[256,256]{1,0:T(8,128)(2,1)} %theta_h.1, f32[1,512]{1,0:T(1,128)} %bitcast.2, s32[1,32,512]{2,1,0:T(8,128)} %rows_h.1, s32[1,32,512]{2,1,0:T(8,128)} %cols_h.1, ...), custom_call_target="tpu_custom_call" | custom-call | tf_op jit(solution)/shard_map/pallas_call | solution.py:450
  77.1 0.8 %shard_map.103 = (bf16[128,256]{1,0:T(8,128)(2,1)}, bf16[128,256]{1,0:T(8,128)(2,1)}, f32[256,256]{1,0:T(8,128)}, f32[1,512]{1,0:T(1,128)}) custom-call(bf16[128,256]{1,0:T(8,128)(2,1)S(1)} %get-tuple-element.12.a, bf16[128,256]{1,0:T(8,128)(2,1)S(1)} %get-tuple-element.13.b, f32[256,256]{1,0:T(8,128)S(1)} %get-tuple-element.14.c, ...), custom_call_target="tpu_custom_call" | custom-call | tf_op jit(solution)/shard_map/pallas_call | solution.py:517

commit v5 on v4

--- a/solution.py
+++ b/solution.py
@@ -1,3 +1,5 @@
+import functools
+
 import jax
 import jax.numpy as jnp
 from jax import lax
@@ -11,7 +13,7 @@
 MESH = pl.DeviceIdType.MESH
 NT = (((1,), (1,)), ((), ()))
 NN = (((1,), (0,)), ((), ()))
-N_SEM = 48
+N_SEM = 73
 
 
 def dot(a, b, dims):
@@ -27,7 +29,7 @@
     feat_h, theta_h, sw_h, rows_h, cols_h, counts_h, cot_h,
     act_o, gf_o, gt_o, gw_o,
     feat, theta, rows, cols, counts, cot,
-    HT, HS, DS, DR, D1, DX, D2, DP, DW, DT, SW, INV, XF, SC, G, GR, LF, LB, LR, GH, GL, GATH, MT, PF, PB,
+    HT, HS, DS, DR, D1, DX, D2, DP, DW, DT, SW, INV, XF, XB, SC, G, GR, LF, LB, LR, GH, GL, GATH, MT, PF, PB,
     RB, ACC, YS, YR, A2, XR, AS, AR, FS, FR, TH,
     T0, TP, TX, T3, TS, ssem, rsem, lsem,
 ):
@@ -70,6 +72,7 @@
         return dev(xh, xl, z, mod4(y + d))
 
     plane = [(a, b) for a in range(4) for b in range(4) if a or b]
+    plane.sort(key=lambda ab: -(min(ab[0], 4 - ab[0]) + min(ab[1], 4 - ab[1])))
     plane_dev = [dev(xh, xl, mod4(z + a), mod4(y + b)) for a, b in plane]
     pair_z = [dev(1 - xh, 1 - xl, mod4(z + d), y) for d in range(4)]
     pair_y = [dev(1 - xh, 1 - xl, z, mod4(y + d)) for d in range(4)]
@@ -122,20 +125,19 @@
 
     loads[0].wait()
     for p in range(2):
-        XF[0, p, xh, z, y] = feat[pl.ds(pl.multiple_of(half + 32 * p, 32), 32), :]
+        XF[p, xh, z, y] = feat[pl.ds(pl.multiple_of(half + 32 * p, 32), 32), :]
 
     pl.semaphore_wait(barrier, len(peers))
 
-    def all_gather(ph, p, lines=None):
-        buf = XF.at[ph, p]
+    def all_gather(buf, p):
         near_dev, pair_dev, ring_dev = (y_dev, pair_y, z_dev) if p == 0 else (z_dev, pair_z, y_dev)
 
         def line(a):
             return buf.at[a, z] if p == 0 else buf.at[a, :, y]
 
         own = buf.at[xh, z, y]
-        same = send_all(buf.at[0, 0, 0:3], [(own, own, near_dev(d)) for d in (1, 3, 2)])
-        pair = send_all(buf.at[0, 0], [(own, own, pair_dev[d]) for d in (0, 1, 3, 2)])
+        same = send_all(buf.at[0, 0, 0:3], [(own, own, near_dev(d)) for d in (2, 1, 3)])
+        pair = send_all(buf.at[0, 0], [(own, own, pair_dev[d]) for d in (2, 1, 3, 0)])
         rings = {d: open_group(buf.at[0, 0:2]) for d in (1, 3, 2)}
         yield
         for stage, a in ((same, xh), (pair, 1 - xh)):
@@ -176,7 +178,7 @@
 
     degrees = degree_sum()
     step([degrees])
-    gathers = [all_gather(0, 0), all_gather(0, 1)]
+    gathers = [all_gather(XF.at[p], p) for p in range(2)]
     step(gathers)
     loads[3].wait()
 
@@ -223,7 +225,6 @@
                     SC[p, a, b, c] = jnp.broadcast_to(column[p * 32:p * 32 + 32], (32, 128))
 
     own_scale = jnp.concatenate([SC[p, xh, z, y] for p in range(2)], axis=0)
-    own_scale = jnp.concatenate([own_scale, own_scale], axis=1)
 
     def table_rows(p, i, k):
         ref = HT.at[core, p] if k == 0 else HS.at[p]
@@ -236,56 +237,39 @@
     def line_of(ref, p, a, i):
         return ref[p, a, i] if p == 0 else ref[p, a, :, i]
 
-    def gather_line(ph, p, i):
+    def scaled_line(p, i):
         pieces = []
         for a in range(2):
-            v = line_of(XF.at[ph], p, a, i).reshape(128, 256)
-            if ph == 0:
-                scale = line_of(SC, p, a, i).reshape(128, 128)
-                v = (v.astype(F32) * jnp.concatenate([scale, scale], axis=1)).astype(BF16)
-            pieces.append(v)
+            v = line_of(XF, p, a, i).reshape(128, 256)
+            scale = line_of(SC, p, a, i).reshape(128, 128)
+            pieces.append((v.astype(F32) * jnp.concatenate([scale, scale], axis=1)).astype(BF16))
         xt = jnp.concatenate(pieces, axis=0).T
-        if ph == 0:
-            xt = jnp.concatenate([xt, jnp.ones((16, 256), BF16)], axis=0)
-        return xt
-
-    def gather_sections(ph, gathers):
-        width = 272 if ph == 0 else 256
-        exchange = []
-        for k in range(2):
-            v = None
-            for p, i in enumerate((z, y)):
-                t = dot(gather_line(ph, p, i), table_rows(p, i, k), NN)
-                v = t if v is None else v + t
-            G[ph, k, 0:width] = v
-        for d in (3, 1):
-            step(gathers)
-            for p, i in enumerate((mod4(z + d), mod4(y + d))):
-                xt = gather_line(ph, p, i)
-                for k in range(2):
-                    G[ph, k, 0:width] += dot(xt, table_rows(p, i, k), NN)
-        if ph == 1:
-            exchange.append(send_all(GR.at[1, :, 0:256], [(G.at[1, :, 0:256], GR.at[1, :, 0:256], sib)]))
-        step(gathers)
-        last = [(0, mod4(z + 2)), (1, mod4(y + 2))]
-        xts = [gather_line(ph, p, i) for p, i in last]
-        for k in (1, 0):
-            v = None
-            for (p, i), xt in zip(last, xts):
-                t = dot(xt, table_rows(p, i, k), NN)
-                v = t if v is None else v + t
-            if ph == 0:
-                G[0, k] += v
-                exchange.append(core_sum(G.at[0, k], GR.at[0, k]))
-            else:
-                LF[k] = v
-                LB[k] = v.astype(BF16)
-                exchange.append(core_sum(LB.at[k], LR.at[k]))
-        return exchange
+        return jnp.concatenate([xt, jnp.ones((16, 256), BF16)], axis=0)
+
+    def back_line(q, p, i):
+        pieces = [line_of(XB.at[q], p, a, i).reshape(128, 128) for a in range(2)]
+        return jnp.concatenate(pieces, axis=0).T
+
+    def lines_dot(line, d, k):
+        total = None
+        for p, i in enumerate((mod4(z + d), mod4(y + d))):
+            t = dot(line(p, i), table_rows(p, i, k), NN)
+            total = t if total is None else total + t
+        return total
 
     arrived(table_group)
     arrived(sw_group)
-    exchange = gather_sections(0, gathers)
+    for k in range(2):
+        G[0, k] = lines_dot(scaled_line, 0, k)
+    for d in (3, 1):
+        step(gathers)
+        for k in range(2):
+            G[0, k] += lines_dot(scaled_line, d, k)
+    step(gathers)
+    exchange = []
+    for k in (1, 0):
+        G[0, k] += lines_dot(scaled_line, 2, k)
+        exchange.append(core_sum(G.at[0, k], GR.at[0, k]))
     for k in (0, 1):
         arrived(exchange[k])
         g = G[0, k] + GR[0, 1 - k]
@@ -299,20 +283,25 @@
             GATH[...] = gathered
         MT[0, k] = ((SW[k] * inverse) * gathered).astype(BF16)
 
-    def reduce_scatter(ph, out):
+    lanes = [slice(q * 128, q * 128 + 128) for q in range(2)]
+
+    def reduce_scatter(ph, q, out):
         rings = [(z_dev, y_dev, z, y), (y_dev, z_dev, y, z)]
+        pb, rb, ys, yr, a2, xr = [ref.at[ph, q] for ref in (PB, RB, YS, YR, A2, XR)]
+        pf, acc = PF.at[q], ACC.at[q]
+        rhs = [MT[ph, k, lanes[q], :] for k in range(2)]
 
         def term(p, i):
-            return dot(table_rows(p, i, 0), MT[ph, 0], NT) + dot(table_rows(p, i, 1), MT[ph, 1], NT)
-
-        ring_groups = [open_group(RB.at[ph, p]) for p in range(2)]
+            return dot(table_rows(p, i, 0), rhs[0], NT) + dot(table_rows(p, i, 1), rhs[1], NT)
+
+        ring_groups = [open_group(rb.at[p]) for p in range(2)]
         for m, d in enumerate((2, 1, 3)):
             for p in range(2):
                 ring_dev, _, ring, _ = rings[p]
-                PB[ph, p, m] = term(p, mod4(ring + d)).astype(BF16).reshape(2, 4, 32, 256)
-                send(ring_groups[p], PB.at[ph, p, m], RB.at[ph, p, m], ring_dev(d))
+                pb[p, m] = term(p, mod4(ring + d)).astype(BF16).reshape(2, 4, 32, 128)
+                send(ring_groups[p], pb.at[p, m], rb.at[p, m], ring_dev(d))
         for p in range(2):
-            PF[p] = term(p, rings[p][2]).reshape(2, 4, 32, 256)
+            pf[p] = term(p, rings[p][2]).reshape(2, 4, 32, 128)
         yield
         axis_groups = []
         for p in range(2):
@@ -320,14 +309,14 @@
             arrived(ring_groups[p])
             for o in range(4):
                 for a in range(2):
-                    v = PF[p, a, o]
+                    v = pf[p, a, o]
                     for m in range(3):
-                        v = v + RB[ph, p, m, a, o].astype(F32)
-                    ACC[p, o, a] = v
-                    YS[ph, p, o, a] = v.astype(BF16)
+                        v = v + rb[p, m, a, o].astype(F32)
+                    acc[p, o, a] = v
+                    ys[p, o, a] = v.astype(BF16)
             axis_groups.append(send_all(
-                YR.at[ph, p],
-                [(YS.at[ph, p, mod4(axis + d)], YR.at[ph, p, d - 1], axis_dev(d)) for d in (2, 1, 3)],
+                yr.at[p],
+                [(ys.at[p, mod4(axis + d)], yr.at[p, d - 1], axis_dev(d)) for d in (2, 1, 3)],
             ))
         yield
         x_groups = []
@@ -335,57 +324,98 @@
             axis = rings[p][3]
             arrived(axis_groups[p])
             for a in range(2):
-                v = ACC[p, axis, a]
+                v = acc[p, axis, a]
                 for i in range(3):
-                    v = v + YR[ph, p, i, a].astype(F32)
-                A2[ph, p, a] = v.astype(BF16)
-            slot = XR.at[ph, p, myx]
-            x_groups.append(send_all(XR.at[ph, p, 0:3], [
-                (A2.at[ph, p, 1 - xh], slot, x_far),
-                (A2.at[ph, p, 1 - xh], slot, x_pair),
-                (A2.at[ph, p, xh], slot, x_same),
+                    v = v + yr[p, i, a].astype(F32)
+                a2[p, a] = v.astype(BF16)
+            slot = xr.at[p, myx]
+            x_groups.append(send_all(xr.at[p, 0:3], [
+                (a2.at[p, 1 - xh], slot, x_far),
+                (a2.at[p, 1 - xh], slot, x_pair),
+                (a2.at[p, xh], slot, x_same),
             ]))
-            XR[ph, p, myx] = A2[ph, p, xh]
+            xr[p, myx] = a2[p, xh]
         yield
         for p in range(2):
             arrived(x_groups[p])
-            terms = [XR[ph, p, i].astype(F32) for i in range(4)]
+            terms = [xr[p, i].astype(F32) for i in range(4)]
             out[p] = (terms[0] + terms[1]) + (terms[2] + terms[3])
             yield
 
-    collected = {}
-    flow = reduce_scatter(0, collected)
-    next(flow)
-    next(flow)
-    next(flow)
+    collected = [{}, {}]
+    flows = [reduce_scatter(0, q, collected[q]) for q in range(2)]
+    for _ in range(3):
+        step(flows)
     back = []
-    for p in range(2):
-        next(flow)
-        part = slice(p * 32, p * 32 + 32)
-        preact = own_scale[part] * collected[p]
-        sig = 1.0 / (1.0 + jnp.exp(-preact))
-        AS[part, :] = (preact * sig).astype(BF16)
-        upstream = cot[pl.ds(pl.multiple_of(half + p * 32, 32), 32), :].astype(F32)
-        grad = upstream * sig * (1.0 + preact * (1.0 - sig))
-        XF[1, p, xh, z, y] = (own_scale[part] * grad).astype(BF16)
-        back.append(all_gather(1, p))
-        step([back[p]])
+    for q in range(2):
+        back.append([])
+        for p in range(2):
+            next(flows[q])
+            part = slice(p * 32, p * 32 + 32)
+            preact = own_scale[part] * collected[q][p]
+            sig = 1.0 / (1.0 + jnp.exp(-preact))
+            AS[part, lanes[q]] = (preact * sig).astype(BF16)
+            upstream = cot[pl.ds(pl.multiple_of(half + p * 32, 32), 32), lanes[q]].astype(F32)
+            grad = upstream * sig * (1.0 + preact * (1.0 - sig))
+            XB[q, p, xh, z, y] = (own_scale[part] * grad).astype(BF16)
+            back[q].append(all_gather(XB.at[q, p], p))
+            step([back[q][p]])
     act_group = send_all(AR, [(AS, AR, sib)])
-    step(back)
-    step(back)
+    for _ in range(2):
+        for q in range(2):
+            step(back[q])
     act_o[pl.ds(half, 64), :] = AS[...]
     arrived(act_group)
     act_o[pl.ds(other_half, 64), :] = AR[...]
-    exchange = gather_sections(1, back)
-    arrived(exchange[0])
-    for k in (0, 1):
-        early = G[1, k, 0:256] + GR[1, 1 - k, 0:256]
-        arrived(exchange[1 + k])
-        g = early + (LF[k] + LR[1 - k].astype(F32))
-        if k == 0:
-            gw_o[...] = jnp.sum(GATH[...] * g, axis=0, keepdims=True) * INV[0]
-        MT[1, k] = ((SW[k] * INV[k]) * g).astype(BF16)
-
+
+    exchange = [[], []]
+    line_q = [functools.partial(back_line, q) for q in range(2)]
+
+    def early_lines(q, d):
+        if d:
+            step(back[q])
+        for k in range(2):
+            v = lines_dot(line_q[q], d, k)
+            if d:
+                v = v + G[1, k, lanes[q]]
+            G[1, k, lanes[q]] = v
+
+    def early_exchange(q):
+        exchange[q].append(core_sum(G.at[1, :, lanes[q]], GR.at[1, :, lanes[q]]))
+
+    def last_lines(q):
+        step(back[q])
+        for k in (1, 0):
+            v = lines_dot(line_q[q], 2, k)
+            LF[k, lanes[q]] = v
+            LB[q, k] = v.astype(BF16)
+            exchange[q].append(core_sum(LB.at[q, k], LR.at[q, k]))
+
+    weight_terms = []
+
+    def back_messages(q):
+        arrived(exchange[q][0])
+        for k in range(2):
+            early = G[1, k, lanes[q]] + GR[1, 1 - k, lanes[q]]
+            arrived(exchange[q][1 + k])
+            g = early + (LF[k, lanes[q]] + LR[q, 1 - k].astype(F32))
+            if k == 0:
+                weight_terms.append(jnp.sum(GATH[lanes[q]] * g, axis=0, keepdims=True))
+            MT[1, k, lanes[q], :] = ((SW[k] * INV[k]) * g).astype(BF16)
+
+    for d in (0, 3):
+        for q in range(2):
+            early_lines(q, d)
+    for q in range(2):
+        early_lines(q, 1)
+        early_exchange(q)
+    collected = [{}, {}]
+    flows = [reduce_scatter(1, q, collected[q]) for q in range(2)]
+    last_lines(0)
+    back_messages(0)
+    last_lines(1)
+    next(flows[0])
+    back_messages(1)
     mine = pl.ds(pl.multiple_of(core * 128, 128), 128)
     theirs = pl.ds(pl.multiple_of((1 - core) * 128, 128), 128)
     v = jnp.zeros((128, 256), F32)
@@ -396,36 +426,42 @@
         TP,
         [(T0.at[mod4(z + a), mod4(y + b)], TP.at[i], plane_dev[i]) for i, (a, b) in enumerate(plane)],
     )
-    collected = {}
-    flow = reduce_scatter(1, collected)
-    next(flow)
+    next(flows[1])
+    gw_o[...] = (weight_terms[0] + weight_terms[1]) * INV[0]
+
+    next(flows[0])
     arrived(theta_group)
     v = T0[z, y]
     for i in range(15):
         v = v + TP[i]
     TX[myx] = v
     theta_group = send_all(TX.at[0:3], [(TX.at[myx], TX.at[myx], d) for d in (x_far, x_pair, x_same)])
-    next(flow)
+    next(flows[1])
+    next(flows[0])
     arrived(theta_group)
     T3[z, y] = (TX[0] + TX[1]) + (TX[2] + TX[3])
     theta_group = send_all(TP, [(T3.at[z, y], T3.at[z, y], d) for d in plane_dev])
-    next(flow)
+    next(flows[1])
+    done = len(groups) - 5
+    for g in range(done):
+        whole(g).wait_send()
     arrived(theta_group)
     theta_group = send_all(TS, [(T3, TS, sib)])
     gt_o[mine, :] = T3[...].reshape(128, 256)
     arrived(theta_group)
     gt_o[theirs, :] = TS[...].reshape(128, 256)
     for p in range(2):
-        next(flow)
+        step(flows)
         part = slice(p * 32, p * 32 + 32)
-        hi, lo = split(own_scale[part] * collected[p])
+        proj = jnp.concatenate([own_scale[part] * collected[q][p] for q in range(2)], axis=1)
+        hi, lo = split(proj)
         FS[part, :] = (dot(hi, theta[...], NT) + dot(lo, theta[...], NT)).astype(BF16)
     grad_group = send_all(FR, [(FS, FR, sib)])
     gf_o[pl.ds(half, 64), :] = FS[...]
     arrived(grad_group)
     gf_o[pl.ds(other_half, 64), :] = FR[...]
     assert len(groups) == N_SEM, len(groups)
-    for g in range(len(groups)):
+    for g in range(done, len(groups)):
         whole(g).wait_send()
 
 
@@ -476,25 +512,26 @@
             buf((128, 128), F32),
             buf((2, 1, 512), F32),
             buf((2, 1, 512), F32),
-            buf((2, 2, 2, 4, 4, 32, 256), BF16),
+            buf((2, 2, 4, 4, 32, 256), BF16),
+            buf((2, 2, 2, 4, 4, 32, 128), BF16),
             buf((2, 2, 4, 4, 32, 128), F32),
             buf((2, 2, 272, 512), F32),
             buf((2, 2, 272, 512), F32),
             buf((2, 256, 512), F32),
-            buf((2, 256, 512), BF16),
-            buf((2, 256, 512), BF16),
+            buf((2, 2, 128, 512), BF16),
+            buf((2, 2, 128, 512), BF16),
             buf((2, 256, 512), BF16),
             buf((2, 256, 512), BF16),
             buf((256, 512), F32),
             buf((2, 2, 256, 512), BF16),
-            buf((2, 2, 4, 32, 256), F32),
-            buf((2, 2, 3, 2, 4, 32, 256), BF16),
-            buf((2, 2, 3, 2, 4, 32, 256), BF16),
-            buf((2, 4, 2, 32, 256), F32),
-            buf((2, 2, 4, 2, 32, 256), BF16),
-            buf((2, 2, 3, 2, 32, 256), BF16),
-            buf((2, 2, 2, 32, 256), BF16),
-            buf((2, 2, 4, 32, 256), BF16),
+            buf((2, 2, 2, 4, 32, 128), F32),
+            buf((2, 2, 2, 3, 2, 4, 32, 128), BF16),
+            buf((2, 2, 2, 3, 2, 4, 32, 128), BF16),
+            buf((2, 2, 4, 2, 32, 128), F32),
+            buf((2, 2, 2, 4, 2, 32, 128), BF16),
+            buf((2, 2, 2, 3, 2, 32, 128), BF16),
+            buf((2, 2, 2, 2, 32, 128), BF16),
+            buf((2, 2, 2, 4, 32, 128), BF16),
             buf((64, 256), BF16),
             buf((64, 256), BF16),
             buf((64, 256), BF16),

time: 78 us -> 77.3 us (level)
  Pallas kernels: 77.2 us -> 76.4 us
    pallas_call x1, Pallas kernels: 76.5 us -> 75.6 us  [body(): pl.pallas_call(layer, out_shape=(jax.ShapeDtypeStruct((128, 256), BF16),...]
where the time goes in v5:
time: 77.3 us; the launch traced here: 77.2 us
  Pallas kernels  76.4 us (99%)
  between operations  0.8 us (1%)
    pallas_call x1, Pallas kernels, body(): pl.pallas_call(layer, out_shape=(jax.ShapeDtypeStruct((128, 256), BF16),...  75.6 us

profile of v5, /device:TPU:1, one launch (start us, length us, event | category | flops | bytes accessed | tf_op | source)
XLA Modules:
  0.0 77.2 jit_solution(14476480102954208518)
XLA Ops:
  0.6 75.6 %shard_map.102 = (bf16[128,256]{1,0:T(8,128)(2,1)S(1)}, bf16[128,256]{1,0:T(8,128)(2,1)S(1)}, f32[256,256]{1,0:T(8,128)S(1)}, f32[1,512]{1,0:T(1,128)S(1)}) custom-call(bf16[128,256]{1,0:T(8,128)(2,1)} %feat_h.1, bf16[256,256]{1,0:T(8,128)(2,1)} %theta_h.1, f32[1,512]{1,0:T(1,128)} %bitcast.2, s32[1,32,512]{2,1,0:T(8,128)} %rows_h.1, s32[1,32,512]{2,1,0:T(8,128)} %cols_h.1, ...), custom_call_target="tpu_custom_call" | custom-call | tf_op jit(solution)/shard_map/pallas_call | solution.py:486
  76.2 0.8 %shard_map.103 = (bf16[128,256]{1,0:T(8,128)(2,1)}, bf16[128,256]{1,0:T(8,128)(2,1)}, f32[256,256]{1,0:T(8,128)}, f32[1,512]{1,0:T(1,128)}) custom-call(bf16[128,256]{1,0:T(8,128)(2,1)S(1)} %get-tuple-element.12.a, bf16[128,256]{1,0:T(8,128)(2,1)S(1)} %get-tuple-element.13.b, f32[256,256]{1,0:T(8,128)S(1)} %get-tuple-element.14.c, ...), custom_call_target="tpu_custom_call" | custom-call | tf_op jit(solution)/shard_map/pallas_call | solution.py:554

commit v6 on v5

--- a/solution.py
+++ b/solution.py
@@ -138,14 +138,14 @@
         own = buf.at[xh, z, y]
         same = send_all(buf.at[0, 0, 0:3], [(own, own, near_dev(d)) for d in (2, 1, 3)])
         pair = send_all(buf.at[0, 0], [(own, own, pair_dev[d]) for d in (2, 1, 3, 0)])
-        rings = {d: open_group(buf.at[0, 0:2]) for d in (1, 3, 2)}
+        rings = {d: open_group(buf.at[0, 0:2]) for d in (2, 1, 3)}
         yield
         for stage, a in ((same, xh), (pair, 1 - xh)):
             arrived(stage)
-            for d in (1, 3, 2):
+            for d in (2, 1, 3):
                 send(rings[d], line(a), line(a), ring_dev(d))
             yield
-        for d in (1, 3, 2):
+        for d in (2, 1, 3):
             arrived(rings[d])
             yield
 
@@ -202,14 +202,14 @@
         send(table_group, HT.at[1 - core, :, a, b], HS.at[:, a, b], sib)
 
     step([degrees])
-    for k in range(3):
+    for k in range(2):
         table_line(k)
     step([degrees])
     step(gathers)
     step(gathers)
     loads[4].wait()
     sw_group = send_all(SW.at[1], [(SW.at[0], SW.at[1], sib)])
-    for k in range(3, 8):
+    for k in range(2, 8):
         table_line(k)
     for copy in loads[5:]:
         copy.wait()
@@ -261,14 +261,14 @@
     arrived(sw_group)
     for k in range(2):
         G[0, k] = lines_dot(scaled_line, 0, k)
-    for d in (3, 1):
+    for d in (2, 3):
         step(gathers)
         for k in range(2):
             G[0, k] += lines_dot(scaled_line, d, k)
     step(gathers)
     exchange = []
     for k in (1, 0):
-        G[0, k] += lines_dot(scaled_line, 2, k)
+        G[0, k] += lines_dot(scaled_line, 1, k)
         exchange.append(core_sum(G.at[0, k], GR.at[0, k]))
     for k in (0, 1):
         arrived(exchange[k])
@@ -386,7 +386,7 @@
     def last_lines(q):
         step(back[q])
         for k in (1, 0):
-            v = lines_dot(line_q[q], 2, k)
+            v = lines_dot(line_q[q], 1, k)
             LF[k, lanes[q]] = v
             LB[q, k] = v.astype(BF16)
             exchange[q].append(core_sum(LB.at[q, k], LR.at[q, k]))
@@ -403,11 +403,11 @@
                 weight_terms.append(jnp.sum(GATH[lanes[q]] * g, axis=0, keepdims=True))
             MT[1, k, lanes[q], :] = ((SW[k] * INV[k]) * g).astype(BF16)
 
-    for d in (0, 3):
+    for d in (0, 2):
         for q in range(2):
             early_lines(q, d)
     for q in range(2):
-        early_lines(q, 1)
+        early_lines(q, 3)
         early_exchange(q)
     collected = [{}, {}]
     flows = [reduce_scatter(1, q, collected[q]) for q in range(2)]

time: 77.3 us -> 76.9 us (level)
  no operation moved by 1% of the time
where the time goes in v6:
time: 76.9 us; the launch traced here: 76.7 us
  Pallas kernels  75.9 us (99%)
  between operations  0.8 us (1%)
    pallas_call x1, Pallas kernels, body(): pl.pallas_call(layer, out_shape=(jax.ShapeDtypeStruct((128, 256), BF16),...  75.1 us

profile of v6, /device:TPU:1, one launch (start us, length us, event | category | flops | bytes accessed | tf_op | source)
XLA Modules:
  0.0 76.7 jit_solution(1440925938693744717)
XLA Ops:
  0.6 75.1 %shard_map.102 = (bf16[128,256]{1,0:T(8,128)(2,1)S(1)}, bf16[128,256]{1,0:T(8,128)(2,1)S(1)}, f32[256,256]{1,0:T(8,128)S(1)}, f32[1,512]{1,0:T(1,128)S(1)}) custom-call(bf16[128,256]{1,0:T(8,128)(2,1)} %feat_h.1, bf16[256,256]{1,0:T(8,128)(2,1)} %theta_h.1, f32[1,512]{1,0:T(1,128)} %bitcast.2, s32[1,32,512]{2,1,0:T(8,128)} %rows_h.1, s32[1,32,512]{2,1,0:T(8,128)} %cols_h.1, ...), custom_call_target="tpu_custom_call" | custom-call | tf_op jit(solution)/shard_map/pallas_call | solution.py:486
  75.8 0.8 %shard_map.103 = (bf16[128,256]{1,0:T(8,128)(2,1)}, bf16[128,256]{1,0:T(8,128)(2,1)}, f32[256,256]{1,0:T(8,128)}, f32[1,512]{1,0:T(1,128)}) custom-call(bf16[128,256]{1,0:T(8,128)(2,1)S(1)} %get-tuple-element.12.a, bf16[128,256]{1,0:T(8,128)(2,1)S(1)} %get-tuple-element.13.b, f32[256,256]{1,0:T(8,128)S(1)} %get-tuple-element.14.c, ...), custom_call_target="tpu_custom_call" | custom-call | tf_op jit(solution)/shard_map/pallas_call | solution.py:554
